TPU v7x, 256 devices: a whole 4x4x8 slice. The times are simulated.
256 devices in a mesh: section: 8 (over y, core), seq: 32 (over x, z).
Axes of the slice: x: 4, y: 4, z: 8, core: 2. Of those that a mesh axis runs over, the one named last changes fastest.
Arguments:
- resident_microbatch: bfloat16 [8, 4096, 1024], P('section', 'seq'), may hold values from -36 to 36
- upcoming_amino_ids: int32 [4096], P('seq'), may hold values from 0 to 31
- upcoming_polymer_sizes: int32 [8], replicated, may hold values from 1 to 1024, 4096 in all
- amino_acid_vectors: bfloat16 [32, 1024], replicated, may hold values from -36 to 36
- polymer_vectors: bfloat16 [8, 1024], replicated, may hold values from -3 to 3
- normalizer_scaling: float32 [8, 1024], P('section'), may hold values from 0.25 to 1.75
- entry_projection_matrix: bfloat16 [8, 1024, 3072], P('section'), may hold values from -0.1875 to 0.1875
- convolution_kernels_long: float32 [8, 2, 1024, 4096], P('section', None, 'seq'), may hold values from -4 to 4
- convolution_skip_coefficients: float32 [8, 2, 1024], P('section', None, 'seq'), may hold values from -1 to 1
- exit_projection_matrix: bfloat16 [8, 1024, 1024], P('section'), may hold values from -0.1875 to 0.1875
- adjoint_seeds: bfloat16 [8, 2, 4096, 1024], P('section', None, 'seq'), may hold values from -0.0625 to 0.0625
Outputs:
- passed: bfloat16 [8, 4096, 1024], P('section', 'seq')
- out_grad: float32 [8, 1024, 1024], P('section', 'seq')
All inputs are finite; a program needn't handle non-finite values.
Results may differ from a plain program's by a relative error of at most 0.025.
Values may be sent and summed in bfloat16 or wider, within the bound.
A program may use at most 128 MiB of HBM per device.

v0:
```python
import math

import jax
import jax.numpy as jnp
from jax import lax
from jax.sharding import Mesh
from jax.sharding import PartitionSpec as P

SEQ = ("seq_0", "seq_1")


epsilon = 1e-06


def shifted(value, axis, by):
    peers = lax.axis_size(axis)
    pairs = [(i, i + by) for i in range(peers) if 0 <= i + by < peers]
    return lax.ppermute(value, axis, pairs)


def summed_rows(terms, axes):
    so_far = terms.astype(jnp.bfloat16)
    for axis in axes:
        so_far = lax.psum_scatter(so_far, axis, scatter_dimension=0, tiled=True)
    return so_far.astype(jnp.float32)


def trig_tables(total_len):
    short_len = math.gcd(total_len, 2 ** ((total_len.bit_length() - 1) // 2))
    long_len = total_len // short_len
    index_short = jnp.arange(short_len, dtype=jnp.int32)
    index_long = jnp.arange(long_len, dtype=jnp.int32)
    angle_short = (index_short[:, None] * index_short[None, :] % short_len).astype(jnp.float32) * (
        2.0 * math.pi / short_len
    )
    angle_long = (index_long[:, None] * index_long[None, :] % long_len).astype(jnp.float32) * (
        2.0 * math.pi / long_len
    )
    angle_twist = (index_short[:, None] * index_long[None, :] % total_len).astype(jnp.float32) * (
        2.0 * math.pi / total_len
    )
    return (
        jnp.cos(angle_short),
        jnp.sin(angle_short),
        jnp.cos(angle_long),
        jnp.sin(angle_long),
        jnp.cos(angle_twist),
        jnp.sin(angle_twist),
    )


def forward_spectrum(signal, tables):
    cos_short, sin_short, cos_long, sin_long, cos_twist, sin_twist = tables
    half_rows = cos_short.shape[0] // 2
    blocks = signal.reshape(signal.shape[0], half_rows, cos_long.shape[0])
    real_first = jnp.einsum("kp,cpq->ckq", cos_short[:, :half_rows], blocks)
    imag_first = -jnp.einsum("kp,cpq->ckq", sin_short[:, :half_rows], blocks)
    real_turned = real_first * cos_twist + imag_first * sin_twist
    imag_turned = imag_first * cos_twist - real_first * sin_twist
    real_out = jnp.einsum("ckq,qm->ckm", real_turned, cos_long) + jnp.einsum(
        "ckq,qm->ckm", imag_turned, sin_long
    )
    imag_out = jnp.einsum("ckq,qm->ckm", imag_turned, cos_long) - jnp.einsum(
        "ckq,qm->ckm", real_turned, sin_long
    )
    return (real_out, imag_out)


def inverse_signal(real_in, imag_in, tables):
    cos_short, sin_short, cos_long, sin_long, cos_twist, sin_twist = tables
    half_rows = cos_short.shape[0] // 2
    total_len = cos_short.shape[0] * cos_long.shape[0]
    real_first = jnp.einsum("ckm,mq->ckq", real_in, cos_long) - jnp.einsum(
        "ckm,mq->ckq", imag_in, sin_long
    )
    imag_first = jnp.einsum("ckm,mq->ckq", imag_in, cos_long) + jnp.einsum(
        "ckm,mq->ckq", real_in, sin_long
    )
    real_turned = real_first * cos_twist - imag_first * sin_twist
    imag_turned = imag_first * cos_twist + real_first * sin_twist
    result = jnp.einsum("pk,ckq->cpq", cos_short[:half_rows], real_turned) - jnp.einsum(
        "pk,ckq->cpq", sin_short[:half_rows], imag_turned
    )
    return result.reshape(real_in.shape[0], -1) * (1.0 / total_len)


def long_filter(signal, spectrum, skip_gain, tables):
    real_signal, imag_signal = forward_spectrum(signal, tables)
    real_kernel, imag_kernel = spectrum
    product_real = real_signal * real_kernel - imag_signal * imag_kernel
    product_imag = real_signal * imag_kernel + imag_signal * real_kernel
    return inverse_signal(product_real, product_imag, tables) + skip_gain[:, None] * signal


def run_gated_convolution_block(inputs, network_settings):
    gain, weight_in, spectra, skips, weight_out, tables = network_settings
    model_width = inputs.shape[1]
    values = inputs.astype(jnp.float32)
    inverse_rms = lax.rsqrt(jnp.mean(values * values, axis=1, keepdims=True) + epsilon)
    normed = (values * inverse_rms * gain).astype(jnp.bfloat16)
    projected = lax.dot_general(
        weight_in, normed, (((0,), (1,)), ((), ())), preferred_element_type=jnp.float32
    ).astype(jnp.bfloat16)
    value_rows = projected[:model_width]
    first_gate = projected[model_width : 2 * model_width]
    second_gate = projected[2 * model_width :]
    value_channels, gate_channels = (
        lax.all_to_all(value_rows, SEQ, split_axis=0, concat_axis=1, tiled=True),
        lax.all_to_all(first_gate, SEQ, split_axis=0, concat_axis=1, tiled=True),
    )
    gated_channels = gate_channels.astype(jnp.float32) * long_filter(
        value_channels.astype(jnp.float32), spectra[0], skips[0], tables
    )
    mixed_channels = long_filter(gated_channels, spectra[1], skips[1], tables).astype(jnp.bfloat16)
    mixed_rows = lax.all_to_all(mixed_channels, SEQ, split_axis=1, concat_axis=0, tiled=True)
    hyena_rows = (second_gate.astype(jnp.float32) * mixed_rows.astype(jnp.float32)).astype(
        jnp.bfloat16
    )
    projected_out = lax.dot_general(
        hyena_rows, weight_out, (((0,), (0,)), ((), ())), preferred_element_type=jnp.float32
    )
    return ((values + projected_out).astype(jnp.bfloat16), hyena_rows)


def embed_tokens(upcoming_amino_ids, upcoming_polymer_sizes, amino_acid_vectors, polymer_vectors):
    seq_rows = upcoming_amino_ids.shape[0]
    position = lax.axis_index(SEQ) * seq_rows + jnp.arange(seq_rows, dtype=jnp.int32)
    chain_ends = jnp.cumsum(upcoming_polymer_sizes)[:-1]
    chain_index = jnp.sum((position[:, None] >= chain_ends[None, :]).astype(jnp.int32), axis=1)
    token_onehot = (
        upcoming_amino_ids[:, None]
        == jnp.arange(amino_acid_vectors.shape[0], dtype=jnp.int32)[None, :]
    ).astype(jnp.bfloat16)
    chain_onehot = (
        chain_index[:, None] == jnp.arange(polymer_vectors.shape[0], dtype=jnp.int32)[None, :]
    ).astype(jnp.bfloat16)
    summed = jnp.dot(
        token_onehot, amino_acid_vectors, preferred_element_type=jnp.float32
    ) + jnp.dot(chain_onehot, polymer_vectors, preferred_element_type=jnp.float32)
    return summed.astype(jnp.bfloat16)


def local(
    resident_microbatch,
    upcoming_amino_ids,
    upcoming_polymer_sizes,
    amino_acid_vectors,
    polymer_vectors,
    normalizer_scaling,
    entry_projection_matrix,
    convolution_kernels_long,
    convolution_skip_coefficients,
    exit_projection_matrix,
    adjoint_seeds,
):
    seq_len = convolution_kernels_long.shape[-1]
    tables = trig_tables(2 * seq_len)
    spectra = (
        forward_spectrum(convolution_kernels_long[0, 0], tables),
        forward_spectrum(convolution_kernels_long[0, 1], tables),
    )
    network_settings = (
        normalizer_scaling[0],
        entry_projection_matrix[0],
        spectra,
        convolution_skip_coefficients[0],
        exit_projection_matrix[0],
        tables,
    )
    initial_result, initial_convolution_sweep = run_gated_convolution_block(
        resident_microbatch[0], network_settings
    )
    handed = shifted(initial_result, "section", 1)
    embedded = embed_tokens(
        upcoming_amino_ids, upcoming_polymer_sizes, amino_acid_vectors, polymer_vectors
    )
    second_in = jnp.where(lax.axis_index("section") == 0, embedded, handed)
    passed, second_hyena = run_gated_convolution_block(second_in, network_settings)
    model_width = exit_projection_matrix.shape[1]
    first_term = jnp.dot(
        initial_convolution_sweep, adjoint_seeds[0, 0], preferred_element_type=jnp.float32
    )
    second_term = jnp.dot(second_hyena, adjoint_seeds[0, 1], preferred_element_type=jnp.float32)
    side_by_side = summed_rows(jnp.concatenate([first_term, second_term], axis=1), SEQ)
    out_grad = side_by_side[:, :model_width] + side_by_side[:, model_width:]
    return (passed[None], out_grad[None])


def solution(mesh):
    torus = Mesh(mesh.devices.reshape(mesh.shape["section"], 4, 8), ("section", "seq_0", "seq_1"))
    placed = (
        P("section", SEQ, None),
        P(SEQ),
        P(),
        P(),
        P(),
        P("section", None),
        P("section", None, None),
        P("section", None, SEQ, None),
        P("section", None, SEQ),
        P("section", None, None),
        P("section", None, SEQ, None),
    )
    return jax.shard_map(
        local,
        mesh=torus,
        in_specs=placed,
        out_specs=(P("section", SEQ, None), P("section", SEQ, None)),
        check_vma=False,
    )
```

profile of v0, /device:TPU:8, one launch (start us, length us, event | category | flops | bytes accessed | tf_op | source)
XLA Modules:
  0.0 271.2 jit_solution(3562175778948266922)
XLA Ops:
  7.2 1.2 fusion.99
  8.4 4.0 %fusion.13 = bf16[3072,128]{0,1:T(8,128)(2,1)S(1)} fusion(bf16[1,1024,3072]{2,1,0:T(8,128)(2,1)} %param.17, bf16[1,128,1024]{2,1,0:T(8,128)(2,1)} %param.11, f32[1024]{0:T(1024)} %bitcast.317, f32[128]{0:T(128)S(1)} %add_rsqrt_fusion.1), kind=kOutput, calls=%fused_computation.8 | convolution fusion | flops 806223872 | bytes 7344640 | tf_op jit(solution)/shard_map/dot_general | solution.py:101
  12.4 0.9 copy-done.18
  13.3 0.7 fusion.423
  14.0 0.9 copy.69
  14.9 11.3 %all-to-all-start.1 = ((bf16[32,32,128]{2,1,0:T(8,128)(2,1)}), bf16[32,32,128]{2,1,0:T(8,128)(2,1)S(1)}, u32[]{:S(2)}, u32[]{:S(2)}) async-start(bf16[32,32,128]{2,1,0:T(8,128)(2,1)} %bitcast.9), calls=%async_computation.1 | async-start | bytes 524288 | tf_op jit(solution)/shard_map/all_to_all | solution.py:108
  26.6 1.3 slice_bitcast_fusion
  30.4 1.6 fusion.62
  32.0 1.5 fusion.58
  33.5 1.5 convolution_add_fusion.8
  35.1 1.5 convolution_subtract_fusion.8
  36.6 1.8 copy.67
  38.4 3.3 %convolution_add_fusion.5 = f32[32,64,128]{2,1,0:T(8,128)} fusion(f32[32,64,128]{2,1,0:T(8,128)} %fusion.62, f32[64,32,128]{2,0,1:T(8,128)} %copy-done.1, f32[64,32,128]{2,0,1:T(8,128)S(1)} %convolution_negate_fusion.1, f32[64,128]{1,0:T(8,128)S(1)} %get-tuple-element.28, f32[64,128]{1,0:T(8,128)S(1)} %get-tuple-element.29), kind=kOutput, calls=%fused_computation.38 | convolution fusion | flops 68386816 | bytes 4259840 | tf_op jit(solution)/shard_map/ckq,qm->ckm/dot_general | solution.py:60
  41.7 1.5 convolution_subtract_fusion.5
  43.2 10.1 %all-to-all-start = ((bf16[32,32,128]{2,1,0:T(8,128)(2,1)}), bf16[32,32,128]{2,1,0:T(8,128)(2,1)}, u32[]{:S(2)}, u32[]{:S(2)}) async-start(bf16[32,32,128]{2,1,0:T(8,128)(2,1)} %bitcast.314), calls=%async_computation | async-start | bytes 524288 | tf_op jit(solution)/shard_map/all_to_all | solution.py:109
  54.0 0.6 fusion.119
  54.6 0.6 fusion.120
  55.1 0.6 convolution_add_fusion.9
  56.1 0.9 multiply_subtract_fusion.7
  59.1 1.0 copy-done.12
  60.1 1.1 fusion.94
  61.2 3.8 %all-to-all-done = bf16[32,32,128]{2,1,0:T(8,128)(2,1)} async-done(((bf16[32,32,128]{2,1,0:T(8,128)(2,1)}), bf16[32,32,128]{2,1,0:T(8,128)(2,1)}, u32[]{:S(2)}, u32[]{:S(2)}) %all-to-all-start) | async-done | bytes 262176 | tf_op jit(solution)/shard_map/all_to_all | solution.py:109
  64.9 1.8 fusion.42
  68.0 0.6 fusion.121
  68.6 0.6 convolution_add_fusion.6
  69.5 0.8 multiply_subtract_fusion.4
  73.2 0.8 copy.75
  74.0 5.9 %all-to-all-start.2 = ((bf16[32,32,128]{2,0,1:T(8,128)(2,1)}), bf16[32,32,128]{2,0,1:T(8,128)(2,1)}, u32[]{:S(2)}, u32[]{:S(2)}) async-start(bf16[32,32,128]{2,0,1:T(8,128)(2,1)} %copy.75), calls=%async_computation.2 | async-start | bytes 524288 | tf_op jit(solution)/shard_map/all_to_all | solution.py:115
  80.1 11.0 %all-to-all-done.2 = bf16[32,32,128]{2,0,1:T(8,128)(2,1)} async-done(((bf16[32,32,128]{2,0,1:T(8,128)(2,1)}), bf16[32,32,128]{2,0,1:T(8,128)(2,1)}, u32[]{:S(2)}, u32[]{:S(2)}) %all-to-all-start.2) | async-done | bytes 262176 | tf_op jit(solution)/shard_map/all_to_all | solution.py:115
  91.1 1.8 convert_element_type.367
  92.9 2.0 copy.76
  95.0 2.3 fusion.50
  97.2 2.1 collective-permute-start
  99.5 1.1 fusion.199
  100.6 4.6 %collective-permute-done = bf16[128,1024]{1,0:T(8,128)(2,1)S(1)} collective-permute-done((bf16[128,1024]{1,0:T(8,128)(2,1)}, bf16[128,1024]{1,0:T(8,128)(2,1)S(1)}, u32[]{:S(2)}, u32[]{:S(2)}) %collective-permute-start) | collective-permute-done | bytes 262176 | tf_op jit(solution)/shard_map/ppermute | solution.py:18
  105.5 4.0 %fusion.10 = bf16[3072,128]{0,1:T(8,128)(2,1)S(1)} fusion(bf16[1,1024,3072]{2,1,0:T(8,128)(2,1)} %param.17, f32[128,1024]{1,0:T(8,128)S(1)} %get-tuple-element.27, f32[1024]{0:T(1024)S(1)} %bitcast.318, f32[128]{0:T(128)S(1)} %add_rsqrt_fusion), kind=kOutput, calls=%fused_computation.7 | convolution fusion | flops 806092800 | bytes 7606784 | tf_op jit(solution)/shard_map/dot_general | solution.py:101
  109.6 0.9 copy-done.17
  110.5 0.7 fusion.422
  111.2 0.8 copy.79
  112.0 4.5 %all-to-all-start.4 = ((bf16[32,32,128]{2,1,0:T(8,128)(2,1)}), bf16[32,32,128]{2,1,0:T(8,128)(2,1)S(1)}, u32[]{:S(2)}, u32[]{:S(2)}) async-start(bf16[32,32,128]{2,1,0:T(8,128)(2,1)} %bitcast.316), calls=%async_computation.4 | async-start | bytes 524288 | tf_op jit(solution)/shard_map/all_to_all | solution.py:108
  116.5 1.8 copy.77
  118.3 10.0 %all-to-all-done.4 = bf16[32,32,128]{2,1,0:T(8,128)(2,1)S(1)} async-done(((bf16[32,32,128]{2,1,0:T(8,128)(2,1)}), bf16[32,32,128]{2,1,0:T(8,128)(2,1)S(1)}, u32[]{:S(2)}, u32[]{:S(2)}) %all-to-all-start.4) | async-done | bytes 262176 | tf_op jit(solution)/shard_map/all_to_all | solution.py:108
  128.3 4.7 %all-to-all-start.3 = ((bf16[32,32,128]{2,1,0:T(8,128)(2,1)}), bf16[32,32,128]{2,1,0:T(8,128)(2,1)}, u32[]{:S(2)}, u32[]{:S(2)}) async-start(bf16[32,32,128]{2,1,0:T(8,128)(2,1)} %bitcast.315), calls=%async_computation.3 | async-start | bytes 524288 | tf_op jit(solution)/shard_map/all_to_all | solution.py:109
  134.3 0.6 fusion.123
  134.8 0.6 convolution_add_fusion.3
  135.8 0.8 multiply_subtract_fusion.2
  139.2 1.0 copy-done.11
  140.2 1.1 fusion.80
  141.3 3.1 %all-to-all-done.3 = bf16[32,32,128]{2,1,0:T(8,128)(2,1)} async-done(((bf16[32,32,128]{2,1,0:T(8,128)(2,1)}), bf16[32,32,128]{2,1,0:T(8,128)(2,1)}, u32[]{:S(2)}, u32[]{:S(2)}) %all-to-all-start.3) | async-done | bytes 262176 | tf_op jit(solution)/shard_map/all_to_all | solution.py:109
  144.3 2.1 fusion.43
  148.3 0.6 convolution_add_fusion.1
  149.0 0.8 multiply_subtract_fusion
  152.5 0.8 copy.85
  153.3 6.6 %all-to-all-start.5 = ((bf16[32,32,128]{2,0,1:T(8,128)(2,1)}), bf16[32,32,128]{2,0,1:T(8,128)(2,1)S(1)}, u32[]{:S(2)}, u32[]{:S(2)}) async-start(bf16[32,32,128]{2,0,1:T(8,128)(2,1)} %copy.85), calls=%async_computation.5 | async-start | bytes 524288 | tf_op jit(solution)/shard_map/all_to_all | solution.py:115
  160.3 3.1 %convolution_convert_fusion.1 = bf16[1024,1024]{0,1:T(8,128)(2,1)} fusion(bf16[1,2,128,1024]{3,2,1,0:T(8,128)(2,1)S(1)} %copy-done.21, f32[1024,128]{0,1:T(8,128)S(1)} %copy-done.16, bf16[3072,128]{0,1:T(8,128)(2,1)} %copy-done.18), kind=kOutput, calls=%fused_computation.14 | convolution fusion | flops 269877248 | bytes 3145728 | tf_op jit(solution)/shard_map/dot_general | solution.py:180
  163.4 8.3 %all-to-all-done.5 = bf16[32,32,128]{2,0,1:T(8,128)(2,1)S(1)} async-done(((bf16[32,32,128]{2,0,1:T(8,128)(2,1)}), bf16[32,32,128]{2,0,1:T(8,128)(2,1)S(1)}, u32[]{:S(2)}, u32[]{:S(2)}) %all-to-all-start.5) | async-done | bytes 262176 | tf_op jit(solution)/shard_map/all_to_all | solution.py:115
  171.9 1.9 convolution_convert_fusion
  173.9 2.4 pad_maximum_fusion
  176.4 44.5 %reduce-scatter.5.cloned.1.call-done = bf16[256,2048]{0,1:T(8,128)(2,1)} async-done(((bf16[1024,2048]{0,1:T(8,128)(2,1)}), bf16[256,2048]{0,1:T(8,128)(2,1)}) %reduce-scatter.5.cloned.1.call-update) | async-done | bytes 1048592 | tf_op jit(solution)/shard_map/reduce_scatter | solution.py:24
  220.9 2.3 copy.104
  223.2 2.1 fusion.53
  225.3 36.9 %reduce-scatter.7.cloned.1.call-done = bf16[32,2048]{1,0:T(8,128)(2,1)} async-done(((bf16[256,2048]{1,0:T(8,128)(2,1)}), bf16[32,2048]{1,0:T(8,128)(2,1)}) %reduce-scatter.7.cloned.1.call-update) | async-done | bytes 131088
  262.2 1.2 copy.105
  263.5 0.8 copy.87
  (110 shorter events, 20.6 us)
Async XLA Ops:
  7.2 87.8 %copy-start = (bf16[1,1024,1024]{2,1,0:T(8,128)(2,1)S(1)}, bf16[1,1024,1024]{2,1,0:T(8,128)(2,1)}, u32[]{:S(2)}) copy-start(bf16[1,1024,1024]{2,1,0:T(8,128)(2,1)} %param.20) | copy-start | bytes 6291460
  12.4 0.9 copy-start.18
  14.9 28.3 %all-to-all-start.1 = ((bf16[32,32,128]{2,1,0:T(8,128)(2,1)}), bf16[32,32,128]{2,1,0:T(8,128)(2,1)S(1)}, u32[]{:S(2)}, u32[]{:S(2)}) async-start(bf16[32,32,128]{2,1,0:T(8,128)(2,1)} %bitcast.9), calls=%async_computation.1 | async-start | bytes 524288 | tf_op jit(solution)/shard_map/all_to_all | solution.py:108
  30.4 1.6 copy-start.1
  35.1 6.6 %copy-start.24 = (f32[1,2,32]{2,1,0:T(2,128)S(1)}, f32[1,2,32]{2,1,0:T(2,128)}, u32[]{:S(2)}) copy-start(f32[1,2,32]{2,1,0:T(2,128)} %param.19) | copy-start | bytes 772
  38.4 3.3 %copy-start.2 = (f32[64,32,128]{2,0,1:T(8,128)S(1)}, f32[64,32,128]{2,0,1:T(8,128)}, u32[]{:S(2)}) copy-start(f32[64,32,128]{2,0,1:T(8,128)} %copy-done.1) | copy-start | bytes 3145732
  38.4 3.3 %copy-start.19 = (f32[32,64,128]{2,1,0:T(8,128)S(1)}, f32[32,64,128]{2,1,0:T(8,128)}, u32[]{:S(2)}) copy-start(f32[32,64,128]{2,1,0:T(8,128)} %fusion.58) | copy-start | bytes 3145732
  43.2 21.7 %all-to-all-start = ((bf16[32,32,128]{2,1,0:T(8,128)(2,1)}), bf16[32,32,128]{2,1,0:T(8,128)(2,1)}, u32[]{:S(2)}, u32[]{:S(2)}) async-start(bf16[32,32,128]{2,1,0:T(8,128)(2,1)} %bitcast.314), calls=%async_computation | async-start | bytes 524288 | tf_op jit(solution)/shard_map/all_to_all | solution.py:109
  54.6 1.2 copy-start.6
  54.6 1.5 copy-start.8
  59.1 1.0 copy-start.12
  68.0 1.2 copy-start.3
  68.0 1.5 copy-start.4
  72.5 7.4 %copy-start.26 = (s32[8]{0:T(128)S(1)}, s32[8]{0:T(128)}, u32[]{:S(2)}) copy-start(s32[8]{0:T(128)} %param.13) | copy-start | bytes 100
  72.5 22.5 %copy-start.20 = (bf16[1,128,1024]{2,1,0:T(8,128)(2,1)S(1)}, bf16[1,128,1024]{2,1,0:T(8,128)(2,1)}, u32[]{:S(2)}) copy-start(bf16[1,128,1024]{2,1,0:T(8,128)(2,1)} %param.11) | copy-start | bytes 786436
  72.8 26.6 %copy-start.25 = (s32[128]{0:T(128)S(1)}, s32[128]{0:T(128)}, u32[]{:S(2)}) copy-start(s32[128]{0:T(128)} %param.12) | copy-start | bytes 1540
  73.1 32.0 %copy-start.23 = (bf16[8,1024]{1,0:T(8,128)(2,1)S(1)}, bf16[8,1024]{1,0:T(8,128)(2,1)}, u32[]{:S(2)}) copy-start(bf16[8,1024]{1,0:T(8,128)(2,1)} %param.15) | copy-start | bytes 49156
  73.2 32.4 %copy-start.22 = (f32[1,1024]{1,0:T(1,128)S(1)}, f32[1,1024]{1,0:T(1,128)}, u32[]{:S(2)}) copy-start(f32[1,1024]{1,0:T(1,128)} %param.16) | copy-start | bytes 12292
  74.0 17.2 %all-to-all-start.2 = ((bf16[32,32,128]{2,0,1:T(8,128)(2,1)}), bf16[32,32,128]{2,0,1:T(8,128)(2,1)}, u32[]{:S(2)}, u32[]{:S(2)}) async-start(bf16[32,32,128]{2,0,1:T(8,128)(2,1)} %copy.75), calls=%async_computation.2 | async-start | bytes 524288 | tf_op jit(solution)/shard_map/all_to_all | solution.py:115
  97.2 7.9 %collective-permute-start = (bf16[128,1024]{1,0:T(8,128)(2,1)}, bf16[128,1024]{1,0:T(8,128)(2,1)S(1)}, u32[]{:S(2)}, u32[]{:S(2)}) collective-permute-start(bf16[128,1024]{1,0:T(8,128)(2,1)} %fusion.50), channel_id=1, source_target_pairs={{0,32},{32,64},{64,96},{96,128},{128,160},{160,192},{192,224},{1,3... | collective-permute-start | bytes 786440 | tf_op jit(solution)/shard_map/ppermute | solution.py:18
  105.5 5.7 %copy-start.14 = (f32[128,1024]{1,0:T(8,128)}, f32[128,1024]{1,0:T(8,128)S(1)}, u32[]{:S(2)}) copy-start(f32[128,1024]{1,0:T(8,128)S(1)} %get-tuple-element.27) | copy-start | bytes 1572868
  109.5 0.9 copy-start.17
  112.0 16.3 %all-to-all-start.4 = ((bf16[32,32,128]{2,1,0:T(8,128)(2,1)}), bf16[32,32,128]{2,1,0:T(8,128)(2,1)S(1)}, u32[]{:S(2)}, u32[]{:S(2)}) async-start(bf16[32,32,128]{2,1,0:T(8,128)(2,1)} %bitcast.316), calls=%async_computation.4 | async-start | bytes 524288 | tf_op jit(solution)/shard_map/all_to_all | solution.py:108
  128.3 16.0 %all-to-all-start.3 = ((bf16[32,32,128]{2,1,0:T(8,128)(2,1)}), bf16[32,32,128]{2,1,0:T(8,128)(2,1)}, u32[]{:S(2)}, u32[]{:S(2)}) async-start(bf16[32,32,128]{2,1,0:T(8,128)(2,1)} %bitcast.315), calls=%async_computation.3 | async-start | bytes 524288 | tf_op jit(solution)/shard_map/all_to_all | solution.py:109
  134.3 1.2 copy-start.7
  134.3 1.5 copy-start.9
  138.2 1.0 copy-start.10
  139.2 1.0 copy-start.11
  147.7 1.2 copy-start.5
  151.9 8.4 %copy-start.16 = (f32[1024,128]{0,1:T(8,128)S(1)}, f32[1024,128]{0,1:T(8,128)}, u32[]{:S(2)}) copy-start(f32[1024,128]{0,1:T(8,128)} %copy.76) | copy-start | bytes 1572868
  151.9 8.4 %copy-start.21 = (bf16[1,2,128,1024]{3,2,1,0:T(8,128)(2,1)S(1)}, bf16[1,2,128,1024]{3,2,1,0:T(8,128)(2,1)}, u32[]{:S(2)}) copy-start(bf16[1,2,128,1024]{3,2,1,0:T(8,128)(2,1)} %param.21) | copy-start | bytes 1572868
  153.3 18.3 %all-to-all-start.5 = ((bf16[32,32,128]{2,0,1:T(8,128)(2,1)}), bf16[32,32,128]{2,0,1:T(8,128)(2,1)S(1)}, u32[]{:S(2)}, u32[]{:S(2)}) async-start(bf16[32,32,128]{2,0,1:T(8,128)(2,1)} %copy.85), calls=%async_computation.5 | async-start | bytes 524288 | tf_op jit(solution)/shard_map/all_to_all | solution.py:115
  160.0 60.9 %reduce-scatter.5.cloned.1.call-start = ((), (), s32[]{:S(2)}) async-start(), calls=%async_computation.8 | async-start | bytes 5242880 | tf_op jit(solution)/shard_map/reduce_scatter | solution.py:24
  171.9 1.9 copy-start.13
  176.3 46.9 %copy-start.15 = (f32[128,1024]{1,0:T(8,128)S(1)}, f32[128,1024]{1,0:T(8,128)}, u32[]{:S(2)}) copy-start(f32[128,1024]{1,0:T(8,128)} %copy-done.14) | copy-start | bytes 1572868
  176.3 85.9 %reduce-scatter.7.cloned.1.call-start = ((), (), s32[]{:S(2)}) async-start(), calls=%async_computation.9 | async-start | bytes 1179648
Sparse Core Ops, SparseCore 0:
  176.4 44.4 reduce-scatter.4
  223.4 38.7 reduce-scatter.6
where the time goes:
time: 272 us; the launch traced here: 271 us
  waiting for transfers between devices  122 us (45%)
  matrix products  60.6 us (22%)
  starting transfers between devices  45.5 us (17%)
  local copies, waits for them, and re-layouts  21.8 us (8%)
  between operations  14.7 us (5%)
  other arithmetic  6.35 us (2%)
    reduce_scatter x1, waiting for transfers between devices, summed_rows(): so_far = lax.psum_scatter(so_far, axis, scatter_dimension=0, tiled=True)  44.5 us
    unnamed x3, waiting for transfers between devices  36.9 us
    all_to_all x2, waiting for transfers between devices, run_gated_convolution_block(): lax.all_to_all(mixed_channels, SEQ, split_axis=1, concat_axis=0, tiled=True)  19.3 us
    all_to_all x2, starting transfers between devices, run_gated_convolution_block(): lax.all_to_all(value_rows, SEQ, split_axis=0, concat_axis=1, tiled=True)  15.8 us
    all_to_all x2, starting transfers between devices, run_gated_convolution_block(): lax.all_to_all(first_gate, SEQ, split_axis=0, concat_axis=1, tiled=True)  14.7 us
    all_to_all x2, starting transfers between devices, run_gated_convolution_block(): lax.all_to_all(mixed_channels, SEQ, split_axis=1, concat_axis=0, tiled=True)  12.5 us
    unnamed x60, local copies, waits for them, and re-layouts  11.2 us
    all_to_all x2, waiting for transfers between devices, run_gated_convolution_block(): lax.all_to_all(value_rows, SEQ, split_axis=0, concat_axis=1, tiled=True)  10 us
  transfers between devices with their start and end apart: 9, of which 8 were waited for; matrix products, arithmetic and copies ran while one was open for 14% of the time, Pallas kernels for 0%

commit v1 on v0

v1 whole, which is shorter than its diff:
```python
import math

import jax
import jax.numpy as jnp
import numpy as np
from jax import lax
from jax.experimental import pallas as pl
from jax.experimental.pallas import tpu as pltpu
from jax.sharding import Mesh
from jax.sharding import PartitionSpec as P

MESH = pl.DeviceIdType.MESH
F32 = jnp.float32
BF16 = jnp.bfloat16
EPS = 1e-06
LANES = 128
CH = 32


def dft_tables(blocks):
    n = LANES * blocks
    a = np.arange(blocks)[None, :]
    k1 = np.arange(blocks)[:, None]
    first = 2.0 * math.pi * a * (k1 + 0.25) / blocks
    eye = np.eye(8)
    fwd = np.kron(np.concatenate([np.cos(first), -np.sin(first)], axis=0), eye)
    inv = np.kron(np.concatenate([np.cos(first).T, -np.sin(first).T], axis=1), eye)
    q = np.arange(LANES)[None, :]
    twist = np.repeat(2.0 * math.pi * q * (k1 + 0.25) / n, 8, axis=0)
    last = 2.0 * math.pi * (np.arange(LANES)[:, None] * q % LANES) / LANES
    c, s = np.cos(last), np.sin(last)
    g_fwd = np.block([[c, -s], [s, c]])
    g_inv = np.block([[c, s], [-s, c]])
    return (
        jnp.asarray(fwd, BF16),
        jnp.asarray(inv, BF16),
        jnp.asarray(np.stack([np.cos(twist), np.sin(twist)]), F32),
        jnp.asarray(np.stack([g_fwd, g_inv]), BF16),
    )


def dot(a, b):
    return lax.dot_general(a, b, (((1,), (0,)), ((), ())), preferred_element_type=F32)


def body(ns, nx, nz,
         x_ref, ids_ref, sizes_ref, amino_ref, poly_ref, gain_ref, win_hbm, h_hbm, skip_ref, wout_hbm,
         seeds_hbm, fk_ref, fi_ref, tw_ref, g_ref,
         passed_ref, grad_ref,
         win, wout, h, spec, sall, vsend, gsend, vrecv, grecv, msend, mrecv, g2t, hyt, yall, hsend, hrecv,
         emb, tab, rsend, rrecv, part,
         lsem, a2a_s, a2a_r, sh_s, sh_r, y_s, y_r, s_s, s_r, f_s, f_r, z_s, z_r):
    seq = nx * nz
    d = CH * seq
    cw = CH * nz
    rows = 8 * seq
    sec, x, z = lax.axis_index("section"), lax.axis_index("seq_0"), lax.axis_index("seq_1")
    me = x * nz + z
    left, right = lax.rem(x + nx - 1, nx), lax.rem(x + 1, nx)
    after, before = lax.rem(sec + 1, ns), lax.rem(sec + ns - 1, ns)

    local = []
    for p in range(3):
        for j in range(nx):
            local.append(pltpu.make_async_copy(
                win_hbm.at[:, pl.ds((p * nx + j) * cw, cw)], win.at[p, j], lsem.at[p * nx + j]))
    local.append(pltpu.make_async_copy(h_hbm, h, lsem.at[3 * nx]))
    for step in range(2):
        local.append(pltpu.make_async_copy(seeds_hbm.at[step], sall.at[step, x], lsem.at[3 * nx + 1 + step]))
    for j in range(nx):
        local.append(pltpu.make_async_copy(
            wout_hbm.at[:, pl.ds(j * cw, cw)], wout.at[j], lsem.at[3 * nx + 3 + j]))
    for c in local:
        c.start()

    barrier = pltpu.get_barrier_semaphore()

    def greet(i, carry):
        peer = lax.rem(me + i, seq)
        pl.semaphore_signal(barrier, inc=1, device_id=(sec, peer // nz, lax.rem(peer, nz)), device_id_type=MESH)
        return carry

    lax.fori_loop(1, seq, greet, 0)
    pl.semaphore_signal(barrier, inc=1, device_id=(after, x, z), device_id_type=MESH)
    pl.semaphore_signal(barrier, inc=1, device_id=(before, x, z), device_id_type=MESH)

    def far(i):
        half = (i + 1) // 2
        return nz // 2 + half * (1 - 2 * lax.rem(i, 2))

    def block_copy(src, dst, s_idx, r_idx, layer, kind, peer):
        return pltpu.make_async_remote_copy(
            src_ref=src, dst_ref=dst, send_sem=a2a_s.at[layer, kind, s_idx], recv_sem=a2a_r.at[layer, kind, r_idx],
            device_id=(sec, peer // nz, lax.rem(peer, nz)), device_id_type=MESH)

    def send_column(send, recv, layer, kind, xx, own):
        def one(i, carry):
            peer = xx * nz + lax.rem(z + far(i), nz)
            block_copy(send.at[peer], recv.at[me], peer, me, layer, kind, peer).start()
            return carry

        lax.fori_loop(0, nz - 1, one, 0)
        if own:
            recv[me] = send[me]
        else:
            peer = xx * nz + z
            block_copy(send.at[peer], recv.at[me], peer, me, layer, kind, peer).start()

    def wait_blocks(send, recv, layer, kind):
        def one(i, carry):
            peer = lax.rem(me + i, seq)
            block_copy(send.at[peer], recv.at[peer], peer, peer, layer, kind, peer).wait_recv()
            return carry

        lax.fori_loop(1, seq, one, 0)

    def drain_blocks(send, recv, layer, kind):
        def one(i, carry):
            peer = lax.rem(me + i, seq)
            block_copy(send.at[peer], recv.at[peer], peer, peer, layer, kind, peer).wait_send()
            return carry

        lax.fori_loop(1, seq, one, 0)

    orders = [o % nx for o in (2, 1, 3, 0)]

    def half_m(ref, half):
        return lambda i: ref.at[i, pl.ds(16 * half, 16)]

    def send_mixed(layer, half):
        src, dst = half_m(msend, half), half_m(mrecv, half)

        def to(peer):
            block_copy(src(peer), dst(me), peer, me, layer, 2 + half, peer).start()

        for o in orders:
            xx = lax.rem(x + o, nx)

            def one(i, carry):
                to(xx * nz + lax.rem(z + far(i), nz))
                return carry

            lax.fori_loop(0, nz - 1, one, 0)
            if o:
                to(xx * nz + z)
        mrecv[me, 16 * half:16 * half + 16] = msend[me, 16 * half:16 * half + 16]

    def wait_mixed(layer, half, sent):
        src, dst = half_m(msend, half), half_m(mrecv, half)

        def one(i, carry):
            peer = lax.rem(me + i, seq)
            c = block_copy(src(peer), dst(peer), peer, peer, layer, 2 + half, peer)
            if sent:
                c.wait_send()
            else:
                c.wait_recv()
            return carry

        lax.fori_loop(1, seq, one, 0)

    def seed_copy(step, direction):
        return pltpu.make_async_remote_copy(
            src_ref=sall.at[step, x], dst_ref=sall.at[step, x], send_sem=s_s.at[step, direction],
            recv_sem=s_r.at[step, direction], device_id=(sec, (right, left)[direction], z), device_id_type=MESH)

    def seed_arrival(step, direction):
        src = (left, right)[direction]
        return pltpu.make_async_remote_copy(
            src_ref=sall.at[step, src], dst_ref=sall.at[step, src], send_sem=s_s.at[step, direction],
            recv_sem=s_r.at[step, direction], device_id=(sec, (right, left)[direction], z), device_id_type=MESH)

    def forward_copy(step, direction):
        src = (left, right)[direction]
        part_rows = pl.ds(64 * direction, 64)
        return pltpu.make_async_remote_copy(
            src_ref=sall.at[step, src, part_rows], dst_ref=sall.at[step, src, part_rows],
            send_sem=f_s.at[step, direction], recv_sem=f_r.at[step, direction],
            device_id=(sec, (right, left)[direction], z), device_id_type=MESH)

    def forward_arrival(step, direction):
        src = lax.rem(x + 2, nx)
        part_rows = pl.ds(64 * direction, 64)
        return pltpu.make_async_remote_copy(
            src_ref=sall.at[step, src, part_rows], dst_ref=sall.at[step, src, part_rows],
            send_sem=f_s.at[step, direction], recv_sem=f_r.at[step, direction],
            device_id=(sec, (right, left)[direction], z), device_id_type=MESH)

    def forward(xin):
        first = dot(fk_ref[...], xin)
        wc, ws = tw_ref[0], tw_ref[1]
        outs = []
        for k in range(2):
            re, im = first[:rows, LANES * k:LANES * k + LANES], first[rows:, LANES * k:LANES * k + LANES]
            turned = jnp.concatenate([re * wc + im * ws, im * wc - re * ws], axis=1).astype(BF16)
            outs.append(dot(turned, g_ref[0]))
        return outs

    def long_filter(xin, f, pair):
        wc, ws = tw_ref[0], tw_ref[1]
        cols = []
        for k, zz in enumerate(forward(xin)):
            s = spec[f, 2 * pair + k]
            zr, zi, hr, hi = zz[:, :LANES], zz[:, LANES:], s[:, :LANES], s[:, LANES:]
            prod = jnp.concatenate([zr * hr - zi * hi, zr * hi + zi * hr], axis=1).astype(BF16)
            back = dot(prod, g_ref[1])
            br, bi = back[:, :LANES], back[:, LANES:]
            cols.append(jnp.concatenate([br * wc - bi * ws, br * ws + bi * wc], axis=0).astype(BF16))
        return dot(fi_ref[...], jnp.concatenate(cols, axis=1))

    def rows_of(ref, pair):
        v = ref[:, 16 * pair:16 * pair + 16, :].astype(F32)
        return jnp.concatenate([v[:, :8, :].reshape(rows, LANES), v[:, 8:, :].reshape(rows, LANES)], axis=1)

    def skip_tile(f, group):
        row = lax.broadcasted_iota(jnp.int32, (8, LANES), 0)
        out = jnp.zeros((8, LANES), F32)
        for r in range(8):
            out = jnp.where(row == r, skip_ref[f, 8 * group + r], out)
        return out

    def with_skip(y, f, pair, xin):
        gains = jnp.concatenate([skip_tile(f, 2 * pair), skip_tile(f, 2 * pair + 1)], axis=1)
        return y + (xin.reshape(seq, 8, 2 * LANES) * gains[None]).reshape(rows, 2 * LANES)

    def convolve(pair):
        v = rows_of(vrecv, pair)
        y = with_skip(long_filter(v.astype(BF16), 0, pair), 0, pair, v)
        gated = rows_of(grecv, pair) * y
        y = with_skip(long_filter(gated.astype(BF16), 1, pair), 1, pair, gated)
        y = y.reshape(seq, 8, 2 * LANES)
        out = jnp.concatenate([y[:, :, :LANES], y[:, :, LANES:]], axis=1)
        msend[:, 16 * pair:16 * pair + 16, :] = out.astype(BF16)

    def filter_spectra():
        scale = 1.0 / (LANES * seq)
        for f in range(2):
            for pair in range(2):
                cols = []
                for k in range(2):
                    lo = 16 * pair + 8 * k
                    cols.append(jnp.concatenate(
                        [h[f, lo:lo + 8, LANES * a:LANES * a + LANES] for a in range(seq)], axis=0))
                outs = forward(jnp.concatenate(cols, axis=1).astype(BF16))
                for k in range(2):
                    spec[f, 2 * pair + k] = outs[k] * scale

    def embed():
        token = lax.broadcasted_iota(jnp.int32, (LANES, LANES), 0)
        pos = me * LANES + lax.broadcasted_iota(jnp.int32, (LANES, LANES), 1)
        chain = jnp.zeros((LANES, LANES), jnp.int32)
        end = jnp.int32(0)
        for j in range(7):
            end = end + sizes_ref[j]
            chain = chain + jnp.where(pos >= end, 1, 0)
        vocab = amino_ref.shape[0]
        ids = jnp.broadcast_to(ids_ref[...], (LANES, LANES))
        hot = jnp.where(token < vocab, jnp.where(token == ids, 1.0, 0.0), jnp.where(token - vocab == chain, 1.0, 0.0))
        tab[...] = jnp.zeros_like(tab)
        tab[:vocab] = amino_ref[...].astype(F32)
        tab[vocab:vocab + 8] = poly_ref[...].astype(F32)
        emb[...] = dot(hot.astype(F32).T.astype(BF16), tab[...].astype(BF16)).astype(BF16)

    def wait_win(p):
        for j in range(nx):
            local[p * nx + j].wait()

    def layer(k, values):
        normed = (values * lax.rsqrt(jnp.mean(values * values, axis=1, keepdims=True) + EPS) * gain_ref[...]).astype(BF16)
        per = cw // CH
        for p, send, recv in ((0, vsend, vrecv), (1, gsend, grecv)):
            if k == 0:
                wait_win(p)
            for o in orders:
                xx = lax.rem(x + o, nx)
                chunk = dot(normed, win[p, xx]).T.astype(BF16)
                send[pl.ds(xx * per, per)] = chunk.reshape(per, CH, LANES)
                if k == 0 and p == 0 and o == orders[0]:
                    pl.semaphore_wait(barrier, seq + 1)
                send_column(send, recv, k, p, xx, o == 0)
        if k == 0:
            wait_win(2)
        for j in range(nx):
            g2t[pl.ds(j * cw, cw)] = dot(normed, win[2, j]).T.astype(BF16)
        if k == 0:
            local[3 * nx].wait()
            filter_spectra()
            embed()
        wait_blocks(vsend, vrecv, k, 0)
        wait_blocks(gsend, grecv, k, 1)
        if k == 0:
            for step in range(2):
                local[3 * nx + 1 + step].wait()
            seed_copy(0, 0).start()
            seed_copy(0, 1).start()
        else:
            for step in range(2):
                for w in range(2):
                    seed_arrival(step, w).wait_recv()
                    forward_copy(step, w).start()
        for pair in range(2):
            convolve(pair)
            send_mixed(k, pair)
        drain_blocks(vsend, vrecv, k, 0)
        drain_blocks(gsend, grecv, k, 1)
        if k == 0:
            for j in range(nx):
                local[3 * nx + 3 + j].wait()
        else:
            for step in range(2):
                for w in range(2):
                    forward_arrival(step, w).wait_recv()
            grad_of(0)
        for half in range(2):
            wait_mixed(k, half, False)
        for half in range(2):
            wait_mixed(k, half, True)
        hyena = mrecv[...].reshape(d, LANES).astype(F32) * g2t[...].astype(F32)
        hyt[k] = hyena.astype(BF16).reshape(nx, cw, LANES)
        for o in orders:
            if o:
                y_copy(k, lax.rem(x + o, nx)).start()
        yall[k, x] = hyt[k, x]
        return hyena.T.astype(BF16)

    def y_copy(step, xx):
        return pltpu.make_async_remote_copy(
            src_ref=hyt.at[step, xx], dst_ref=yall.at[step, x], send_sem=y_s.at[step, xx], recv_sem=y_r.at[step, x],
            device_id=(sec, xx, z), device_id_type=MESH)

    def y_arrival(step, xx):
        return pltpu.make_async_remote_copy(
            src_ref=hyt.at[step, xx], dst_ref=yall.at[step, xx], send_sem=y_s.at[step, xx], recv_sem=y_r.at[step, xx],
            device_id=(sec, xx, z), device_id_type=MESH)

    def grad_of(step):
        for o in range(1, nx):
            y_arrival(step, lax.rem(x + o, nx)).wait_recv()
        y = jnp.concatenate([yall[step, j] for j in range(nx)], axis=1)
        half_d = d // 2
        for n in range(2):
            cols = slice(n * half_d, (n + 1) * half_d)
            s = jnp.concatenate([sall[step, j, :, cols] for j in range(nx)], axis=0)
            term = dot(y, s)
            if step == 0:
                part[:, cols] = term
            else:
                part[:, cols] = part[:, cols] + term

    def shift_copy(j):
        return pltpu.make_async_remote_copy(
            src_ref=hsend.at[j], dst_ref=hrecv.at[j], send_sem=sh_s.at[j], recv_sem=sh_r.at[j],
            device_id=(after, x, z), device_id_type=MESH)

    first_in = x_ref[...].astype(F32)
    hyena_rows = layer(0, first_in)
    for j in range(nx):
        out = x_ref[:, j * cw:(j + 1) * cw].astype(F32) + dot(hyena_rows, wout[j])
        hsend[j] = out.astype(BF16)
        shift_copy(j).start()
    seed_copy(1, 0).start()
    seed_copy(1, 1).start()
    for j in range(nx):
        shift_copy(j).wait_recv()
    handed = jnp.concatenate([hrecv[j] for j in range(nx)], axis=1)
    head = lax.broadcast(sec, (LANES, d)) == 0
    second_in = jnp.where(head, emb[...].astype(F32), handed.astype(F32))
    emb[...] = second_in.astype(BF16)
    hyena_rows = layer(1, second_in)
    for j in range(nx):
        cols = slice(j * cw, (j + 1) * cw)
        passed_ref[:, cols] = (emb[:, cols].astype(F32) + dot(hyena_rows, wout[j])).astype(BF16)
    grad_of(1)

    def z_copy(zz, to):
        return pltpu.make_async_remote_copy(
            src_ref=rsend.at[zz], dst_ref=rrecv.at[z if to else zz], send_sem=z_s.at[zz],
            recv_sem=z_r.at[z if to else zz], device_id=(sec, x, zz), device_id_type=MESH)

    rsend[...] = part[...].astype(BF16).reshape(nz, CH, d)

    def z_send(i, carry):
        z_copy(lax.rem(z + far(i), nz), True).start()
        return carry

    lax.fori_loop(0, nz - 1, z_send, 0)
    grad_ref[...] = part[pl.ds(pl.multiple_of(z * CH, CH), CH), :]

    for j in range(nx):
        shift_copy(j).wait_send()
    for step in range(2):
        for w in range(2):
            seed_copy(step, w).wait_send()
            forward_copy(step, w).wait_send()
        for o in range(1, nx):
            y_copy(step, lax.rem(x + o, nx)).wait_send()

    def z_wait(i, carry):
        zz = lax.rem(z + i, nz)
        z_copy(zz, False).wait_recv()
        grad_ref[...] = grad_ref[...] + rrecv[zz].astype(F32)
        return carry

    lax.fori_loop(1, nz, z_wait, 0)

    def z_drain(i, carry):
        z_copy(lax.rem(z + i, nz), True).wait_send()
        return carry

    lax.fori_loop(1, nz, z_drain, 0)


def local(shape, resident, ids, sizes, amino, poly, gain, win, kernels, skips, wout, seeds):
    ns, nx, nz = shape
    seq = nx * nz
    d = CH * seq
    cw = CH * nz
    fk, fi, tw, g = dft_tables(seq)
    vmem = pl.BlockSpec(memory_space=pltpu.VMEM)
    smem = pl.BlockSpec(memory_space=pltpu.SMEM)
    hbm = pl.BlockSpec(memory_space=pl.ANY)
    dma = pltpu.SemaphoreType.DMA
    passed, grad = pl.pallas_call(
        lambda *refs: body(ns, nx, nz, *refs),
        out_shape=(jax.ShapeDtypeStruct((LANES, d), BF16), jax.ShapeDtypeStruct((CH, d), F32)),
        in_specs=[vmem, vmem, smem, vmem, vmem, vmem, hbm, hbm, smem, hbm, hbm, vmem, vmem, vmem, vmem],
        out_specs=(vmem, vmem),
        scratch_shapes=[
            pltpu.VMEM((3, nx, d, cw), BF16),
            pltpu.VMEM((nx, d, cw), BF16),
            pltpu.VMEM((2, CH, LANES * seq), F32),
            pltpu.VMEM((2, 4, 8 * seq, 2 * LANES), F32),
            pltpu.VMEM((2, nx, LANES, d), BF16),
            pltpu.VMEM((seq, CH, LANES), BF16),
            pltpu.VMEM((seq, CH, LANES), BF16),
            pltpu.VMEM((seq, CH, LANES), BF16),
            pltpu.VMEM((seq, CH, LANES), BF16),
            pltpu.VMEM((seq, CH, LANES), BF16),
            pltpu.VMEM((seq, CH, LANES), BF16),
            pltpu.VMEM((d, LANES), BF16),
            pltpu.VMEM((2, nx, cw, LANES), BF16),
            pltpu.VMEM((2, nx, cw, LANES), BF16),
            pltpu.VMEM((nx, LANES, cw), BF16),
            pltpu.VMEM((nx, LANES, cw), BF16),
            pltpu.VMEM((LANES, d), BF16),
            pltpu.VMEM((LANES, d), F32),
            pltpu.VMEM((nz, CH, d), BF16),
            pltpu.VMEM((nz, CH, d), BF16),
            pltpu.VMEM((cw, d), F32),
            dma((4 * nx + 3,)),
            dma((2, 4, seq)),
            dma((2, 4, seq)),
            dma((nx,)),
            dma((nx,)),
            dma((2, nx)),
            dma((2, nx)),
            dma((2, 2)),
            dma((2, 2)),
            dma((2, 2)),
            dma((2, 2)),
            dma((nz,)),
            dma((nz,)),
        ],
        compiler_params=pltpu.CompilerParams(
            collective_id=0, has_side_effects=True, vmem_limit_bytes=60 * 1024 * 1024),
    )(resident[0], ids.reshape(1, LANES), sizes, amino, poly, gain, win[0], kernels[0], skips[0], wout[0],
      seeds[0], fk, fi, tw, g)
    return passed[None], grad[None]


SEQ = ("seq_0", "seq_1")


def build(mesh, ns, nx, nz):
    torus = Mesh(mesh.devices.reshape(ns, nx, nz), ("section", "seq_0", "seq_1"))
    placed = (
        P("section", SEQ, None),
        P(SEQ),
        P(),
        P(),
        P(),
        P("section", None),
        P("section", None, None),
        P("section", None, SEQ, None),
        P("section", None, SEQ),
        P("section", None, None),
        P("section", None, SEQ, None),
    )
    return jax.shard_map(
        lambda *args: local((ns, nx, nz), *args),
        mesh=torus,
        in_specs=placed,
        out_specs=(P("section", SEQ, None), P("section", SEQ, None)),
        check_vma=False,
    )


def solution(mesh):
    return build(mesh, mesh.shape["section"], 4, 8)
```

time: 272 us -> 92.5 us (0.34)
  waiting for transfers between devices: 122 us -> 0 us
  Pallas kernels: 0 us -> 88.4 us
  matrix products: 60.6 us -> 0 us
  starting transfers between devices: 45.5 us -> 0 us
  local copies, waits for them, and re-layouts: 21.8 us -> 3.24 us
  between operations: 14.7 us -> 0.64 us
  other arithmetic: 6.35 us -> 0 us
    pallas_call x0 -> x1, Pallas kernels: none -> 88.4 us  [local(): pl.pallas_call(lambda *refs: body(ns, nx, nz, *refs), out_shape=(jax.Shap...]
    dot_general x68 -> x0, matrix products: 60.6 us -> none  [the longest x2 7.97 us: run_gated_convolution_block(): lax.dot_general(weight_in, normed, (((0,), (1,)), ((), ())), preferred_el...]
    reduce_scatter x1 -> x0, waiting for transfers between devices: 44.5 us -> none  [summed_rows(): so_far = lax.psum_scatter(so_far, axis, scatter_dimension=0, tiled=True)]
    all_to_all x6 -> x0, starting transfers between devices: 43.1 us -> none  [the longest x2 15.8 us: run_gated_convolution_block(): lax.all_to_all(value_rows, SEQ, split_axis=0, concat_axis=1, tiled=True)]
    unnamed x3 -> x0, waiting for transfers between devices: 36.9 us -> none
    all_to_all x6 -> x0, waiting for transfers between devices: 36.2 us -> none  [the longest x2 19.3 us: run_gated_convolution_block(): lax.all_to_all(mixed_channels, SEQ, split_axis=1, concat_axis=0, tiled=True)]
    unnamed x60 -> x2, local copies, waits for them, and re-layouts: 11.2 us -> 3.24 us
    slice x6 -> x0, local copies, waits for them, and re-layouts: 6.8 us -> none  [the longest x4 5.09 us: run_gated_convolution_block(): first_gate = projected[model_width:2 * model_width]]
  transfers between devices with their start and end apart: 9 -> 0, of which waited for: 8 -> 0; matrix products, arithmetic and copies ran while one was open for 14% -> 0% of each run, Pallas kernels for 0% -> 0%
where the time goes in v1:
time: 92.5 us; the launch traced here: 92.3 us
  Pallas kernels  88.4 us (96%)
  local copies, waits for them, and re-layouts  3.24 us (4%)
    pallas_call x1, Pallas kernels, local(): pl.pallas_call(lambda *refs: body(ns, nx, nz, *refs), out_shape=(jax.Shap...  88.4 us
    unnamed x2, local copies, waits for them, and re-layouts  3.24 us

profile of v1, /device:TPU:8, one launch (start us, length us, event | category | flops | bytes accessed | tf_op | source)
XLA Modules:
  0.0 92.3 jit_solution(11198081850206725062)
XLA Ops:
  0.6 88.4 %shard_map.158 = (bf16[128,1024]{1,0:T(8,128)(2,1)}, f32[32,1024]{1,0:T(8,128)}) custom-call(bf16[128,1024]{1,0:T(8,128)(2,1)} %bitcast.13, s32[1,128]{1,0:T(1,128)} %bitcast.17, s32[8]{0:T(128)} %refs_2_.1, bf16[32,1024]{1,0:T(8,128)(2,1)} %refs_3_.1, bf16[8,1024]{1,0:T(8,128)(2,1)} %refs_4_.1, f32[1,1024]{1,0:T(1,128)} %refs_5_.1, ...), custom_call_target="tpu_custom_call" | custom-call | tf_op jit(solution)/shard_map/pallas_call | solution.py:423
  89.1 1.7 %copy.19 = bf16[1,128,1024]{2,1,0:T(8,128)(2,1)} copy(bf16[1,128,1024]{2,1,0:T(8,128)(2,1)} %bitcast.14) | data formatting | bytes 524288
  90.7 1.6 %copy.20 = f32[1,32,1024]{2,1,0:T(8,128)} copy(f32[1,32,1024]{2,1,0:T(8,128)} %bitcast.15) | data formatting | bytes 262144

commit v2 on v1

v2 whole, which is shorter than its diff:
```python
import math

import jax
import jax.numpy as jnp
import numpy as np
from jax import lax
from jax.experimental import pallas as pl
from jax.experimental.pallas import tpu as pltpu
from jax.sharding import Mesh
from jax.sharding import PartitionSpec as P

MESH = pl.DeviceIdType.MESH
F32 = jnp.float32
BF16 = jnp.bfloat16
EPS = 1e-06
LANES = 128
CH = 32


def dft_tables(blocks):
    n = LANES * blocks
    a = np.arange(blocks)[None, :]
    k1 = np.arange(blocks)[:, None]
    first = 2.0 * math.pi * a * (k1 + 0.25) / blocks
    eye = np.eye(8)
    fwd = np.kron(np.concatenate([np.cos(first), -np.sin(first)], axis=0), eye)
    inv = np.kron(np.concatenate([np.cos(first).T, -np.sin(first).T], axis=1), eye)
    q = np.arange(LANES)[None, :]
    twist = np.repeat(2.0 * math.pi * q * (k1 + 0.25) / n, 8, axis=0)
    last = 2.0 * math.pi * (np.arange(LANES)[:, None] * q % LANES) / LANES
    c, s = np.cos(last), np.sin(last)
    g_fwd = np.block([[c, -s], [s, c]])
    g_inv = np.block([[c, s], [-s, c]])
    return (
        jnp.asarray(fwd, BF16),
        jnp.asarray(inv, BF16),
        jnp.asarray(np.stack([np.cos(twist), np.sin(twist)]), F32),
        jnp.asarray(np.stack([g_fwd, g_inv]), BF16),
    )


def dot(a, b):
    return lax.dot_general(a, b, (((1,), (0,)), ((), ())), preferred_element_type=F32)


def body(ns, nx, nz,
         x_hbm, ids_hbm, sizes_hbm, amino_hbm, poly_hbm, gain_hbm, win_hbm, h_hbm, skip_hbm, wout_hbm,
         seeds_hbm, fk_hbm, fi_hbm, tw_hbm, g_hbm,
         passed_ref, grad_ref,
         x_ref, ids_ref, sizes_ref, amino_ref, poly_ref, gain_ref, skip_ref, fk_ref, fi_ref, tw_ref, g_ref,
         win, wout, h, spec, sall, vg_send, vg_recv, m_send, m_recv, g2t, hyt, yall, hsend, hrecv,
         emb, tab, acc, part, rsend, rrecv,
         lsem, vg_s, vg_r, m_s, m_r, sh_s, sh_r, y_s, y_r, s_s, s_r, f_s, f_r, z_s, z_r):
    seq = nx * nz
    d = CH * seq
    cw = CH * nz
    hw = cw // 2
    rows = 8 * seq
    sec, x, z = lax.axis_index("section"), lax.axis_index("seq_0"), lax.axis_index("seq_1")
    me = x * nz + z
    left, right = lax.rem(x + nx - 1, nx), lax.rem(x + 1, nx)
    after, before = lax.rem(sec + 1, ns), lax.rem(sec + ns - 1, ns)

    copies = {}

    def fetch(name, src, dst):
        copies[name] = pltpu.make_async_copy(src, dst, lsem.at[len(copies)])
        copies[name].start()

    fetch("x", x_hbm, x_ref)
    fetch("gain", gain_hbm, gain_ref)
    for p in range(3):
        for j in range(nx):
            fetch(("win", p, j), win_hbm.at[:, pl.ds((p * nx + j) * cw, cw)], win.at[p, j])

    barrier = pltpu.get_barrier_semaphore()

    def greet(i, carry):
        peer = lax.rem(me + i, seq)
        pl.semaphore_signal(barrier, inc=1, device_id=(sec, peer // nz, lax.rem(peer, nz)), device_id_type=MESH)
        return carry

    pl.semaphore_signal(barrier, inc=1, device_id=(after, x, z), device_id_type=MESH)
    pl.semaphore_signal(barrier, inc=1, device_id=(before, x, z), device_id_type=MESH)
    lax.fori_loop(1, seq, greet, 0)

    fetch("fk", fk_hbm, fk_ref)
    fetch("tw", tw_hbm, tw_ref)
    fetch("g", g_hbm, g_ref)
    fetch("h", h_hbm, h)
    fetch("ids", ids_hbm, ids_ref)
    fetch("sizes", sizes_hbm, sizes_ref)
    fetch("amino", amino_hbm, amino_ref)
    fetch("poly", poly_hbm, poly_ref)
    fetch("skip", skip_hbm, skip_ref)
    fetch("fi", fi_hbm, fi_ref)
    for step in range(2):
        fetch(("seed", step), seeds_hbm.at[step], sall.at[step, x])
    for j in range(nx):
        fetch(("wout", j), wout_hbm.at[:, pl.ds(j * cw, cw)], wout.at[j])

    def far(i):
        half = (i + 1) // 2
        return nz // 2 + half * (1 - 2 * lax.rem(i, 2))

    orders = [o % nx for o in (2, 1, 3, 0)]

    def block_to(peer, src, dst, send_sem, recv_sem):
        pltpu.make_async_remote_copy(
            src_ref=src.at[peer], dst_ref=dst.at[me], send_sem=send_sem, recv_sem=recv_sem,
            device_id=(sec, peer // nz, lax.rem(peer, nz)), device_id_type=MESH).start()

    def send_column(o, src, dst, send_sem, recv_sem):
        xx = lax.rem(x + o, nx)

        def one(i, carry):
            block_to(xx * nz + lax.rem(z + far(i), nz), src, dst, send_sem, recv_sem)
            return carry

        lax.fori_loop(0, nz - 1, one, 0)
        if o:
            block_to(xx * nz + z, src, dst, send_sem, recv_sem)
        else:
            dst[me] = src[me]

    def wait_all(ref, sem):
        block = ref.at[pl.ds(0, seq - 1)]
        pltpu.make_async_copy(block, block, sem).wait()

    def send_vg(k, half, o):
        send_column(o, vg_send.at[half], vg_recv.at[half], vg_s.at[k, half], vg_r.at[k, half])

    def send_mixed(k, half):
        for o in orders:
            send_column(o, m_send.at[half], m_recv.at[half], m_s.at[k, half], m_r.at[k, half])

    def wait_vg(k, half):
        wait_all(vg_recv.at[half], vg_r.at[k, half])

    def wait_mixed(k, half):
        wait_all(m_recv.at[half], m_r.at[k, half])

    def wait_sent(k):
        for half in range(2):
            wait_all(vg_send.at[half], vg_s.at[k, half])
            wait_all(m_send.at[half], m_s.at[k, half])

    def along_x(ref, send_sem, recv_sem, direction):
        return pltpu.make_async_remote_copy(
            src_ref=ref, dst_ref=ref, send_sem=send_sem, recv_sem=recv_sem,
            device_id=(sec, (right, left)[direction], z), device_id_type=MESH)

    def seed_copy(step, w):
        return along_x(sall.at[step, x], s_s.at[step, w], s_r.at[step, w], w)

    def seed_arrival(step, w):
        return along_x(sall.at[step, (left, right)[w]], s_s.at[step, w], s_r.at[step, w], w)

    def forward_copy(step, w):
        return along_x(sall.at[step, (left, right)[w], pl.ds(64 * w, 64)], f_s.at[step, w], f_r.at[step, w], w)

    def forward_arrival(step, w):
        return along_x(sall.at[step, lax.rem(x + 2, nx), pl.ds(64 * w, 64)], f_s.at[step, w], f_r.at[step, w], w)

    def forward(xin):
        first = dot(fk_ref[...], xin)
        wc, ws = tw_ref[0], tw_ref[1]
        outs = []
        for k in range(2):
            re, im = first[:rows, LANES * k:LANES * k + LANES], first[rows:, LANES * k:LANES * k + LANES]
            turned = jnp.concatenate([re * wc + im * ws, im * wc - re * ws], axis=1).astype(BF16)
            outs.append(dot(turned, g_ref[0]))
        return outs

    def long_filter(xin, f, pair):
        wc, ws = tw_ref[0], tw_ref[1]
        cols = []
        for k, zz in enumerate(forward(xin)):
            s = spec[f, 2 * pair + k]
            zr, zi, hr, hi = zz[:, :LANES], zz[:, LANES:], s[:, :LANES], s[:, LANES:]
            prod = jnp.concatenate([zr * hr - zi * hi, zr * hi + zi * hr], axis=1).astype(BF16)
            back = dot(prod, g_ref[1])
            br, bi = back[:, :LANES], back[:, LANES:]
            cols.append(jnp.concatenate([br * wc - bi * ws, br * ws + bi * wc], axis=0).astype(BF16))
        return dot(fi_ref[...], jnp.concatenate(cols, axis=1))

    def rows_of(half, which):
        v = vg_recv[half, :, which].astype(F32)
        return jnp.concatenate([v[:, :8, :].reshape(rows, LANES), v[:, 8:, :].reshape(rows, LANES)], axis=1)

    def skip_tile(f, group):
        row = lax.broadcasted_iota(jnp.int32, (8, LANES), 0)
        out = jnp.zeros((8, LANES), F32)
        for r in range(8):
            out = jnp.where(row == r, skip_ref[f, 8 * group + r], out)
        return out

    def with_skip(y, f, pair, xin):
        gains = jnp.concatenate([skip_tile(f, 2 * pair), skip_tile(f, 2 * pair + 1)], axis=1)
        return y + (xin.reshape(seq, 8, 2 * LANES) * gains[None]).reshape(rows, 2 * LANES)

    def convolve(pair):
        v = rows_of(pair, 0)
        y = with_skip(long_filter(v.astype(BF16), 0, pair), 0, pair, v)
        gated = rows_of(pair, 1) * y
        y = with_skip(long_filter(gated.astype(BF16), 1, pair), 1, pair, gated)
        y = y.reshape(seq, 8, 2 * LANES)
        out = jnp.concatenate([y[:, :, :LANES], y[:, :, LANES:]], axis=1)
        m_send[pair] = out.astype(BF16)

    def filter_spectra(f, pair):
        scale = 1.0 / (LANES * seq)
        cols = []
        for k in range(2):
            lo = 16 * pair + 8 * k
            cols.append(jnp.concatenate(
                [h[f, lo:lo + 8, LANES * a:LANES * a + LANES] for a in range(seq)], axis=0))
        outs = forward(jnp.concatenate(cols, axis=1).astype(BF16))
        for k in range(2):
            spec[f, 2 * pair + k] = outs[k] * scale

    def embed():
        token = lax.broadcasted_iota(jnp.int32, (LANES, LANES), 0)
        pos = me * LANES + lax.broadcasted_iota(jnp.int32, (LANES, LANES), 1)
        chain = jnp.zeros((LANES, LANES), jnp.int32)
        end = jnp.int32(0)
        for j in range(7):
            end = end + sizes_ref[j]
            chain = chain + jnp.where(pos >= end, 1, 0)
        vocab = amino_ref.shape[0]
        ids = jnp.broadcast_to(ids_ref[...], (LANES, LANES))
        hot = jnp.where(token < vocab, jnp.where(token == ids, 1.0, 0.0), jnp.where(token - vocab == chain, 1.0, 0.0))
        tab[...] = jnp.zeros_like(tab)
        tab[:vocab] = amino_ref[...].astype(F32)
        tab[vocab:vocab + 8] = poly_ref[...].astype(F32)
        emb[...] = dot(hot.astype(F32).T.astype(BF16), tab[...].astype(BF16)).astype(BF16)

    per = cw // CH

    def project(p, xx, normed):
        chunk = dot(normed, win[p, xx]).T.astype(BF16).reshape(per, 2, 16, LANES)
        for half in range(2):
            vg_send[half, pl.ds(xx * per, per), p] = chunk[:, half]

    def project_gate(j, normed):
        chunk = dot(normed, win[2, j]).T.astype(BF16).reshape(per, 2, 16, LANES)
        for half in range(2):
            g2t[half, pl.ds(j * hw, hw)] = chunk[:, half].reshape(hw, LANES)

    def y_copy(step, half, xx, to):
        return pltpu.make_async_remote_copy(
            src_ref=hyt.at[step, half, xx], dst_ref=yall.at[step, half, x if to else xx],
            send_sem=y_s.at[step, half, xx], recv_sem=y_r.at[step, half, x if to else xx],
            device_id=(sec, xx, z), device_id_type=MESH)

    def make_hyena(k, half):
        hyena = m_recv[half].reshape(d // 2, LANES).astype(F32) * g2t[half].astype(F32)
        hyt[k, half] = hyena.astype(BF16).reshape(nx, hw, LANES)
        for o in orders:
            if o:
                y_copy(k, half, lax.rem(x + o, nx), True).start()
        yall[k, half, x] = hyt[k, half, x]
        return hyena.T.astype(BF16)

    def wait_y(step, half):
        for o in range(1, nx):
            y_copy(step, half, lax.rem(x + o, nx), False).wait_recv()

    def grad_of(step, half):
        y = jnp.concatenate([yall[step, half, j] for j in range(nx)], axis=1)
        half_d = d // 2
        for n in range(2):
            cols = slice(n * half_d, (n + 1) * half_d)
            s = jnp.concatenate([sall[step, j, :, cols] for j in range(nx)], axis=0)
            term = dot(y, s)
            if step == 0:
                part[half, :, cols] = term
            else:
                part[half, :, cols] = part[half, :, cols] + term

    def exit_rows(half, j):
        w = wout[j].reshape(seq, 2, 16, cw)
        return w[:, half].reshape(d // 2, cw)

    def half_exit(hyena_rows):
        for j in range(nx):
            acc[:, j * cw:(j + 1) * cw] = dot(hyena_rows, exit_rows(0, j))

    def normalize(values):
        return (values * lax.rsqrt(jnp.mean(values * values, axis=1, keepdims=True) + EPS) * gain_ref[...]).astype(BF16)

    def layer(k, normed):
        for o in orders:
            xx = lax.rem(x + o, nx)
            project(0, xx, normed)
            project(1, xx, normed)
            if k == 0 and o == orders[0]:
                pl.semaphore_wait(barrier, seq + 1)
            send_vg(k, 0, o)
        for o in orders:
            send_vg(k, 1, o)
        if k == 1:
            for step in range(2):
                for w in range(2):
                    seed_arrival(step, w).wait_recv()
                    forward_copy(step, w).start()
        else:
            for j in range(nx):
                copies["win", 2, j].wait()
        for j in range(nx):
            project_gate(j, normed)
        if k == 0:
            for name in ("h", "fk", "tw", "g", "fi", "skip", "ids", "sizes", "amino", "poly"):
                copies[name].wait()
            for pair in range(2):
                for f in range(2):
                    filter_spectra(f, pair)
            embed()
        for half in range(2):
            wait_vg(k, half)
            convolve(half)
            send_mixed(k, half)
        if k == 0:
            for step in range(2):
                copies["seed", step].wait()
                seed_copy(step, 0).start()
                seed_copy(step, 1).start()
            for j in range(nx):
                copies["wout", j].wait()
        else:
            for step in range(2):
                for w in range(2):
                    forward_arrival(step, w).wait_recv()
            for half in range(2):
                wait_y(0, half)
                grad_of(0, half)
        wait_mixed(k, 0)
        first_rows = make_hyena(k, 0)
        half_exit(first_rows)
        wait_mixed(k, 1)
        return make_hyena(k, 1)

    def shift_copy(j):
        return pltpu.make_async_remote_copy(
            src_ref=hsend.at[j], dst_ref=hrecv.at[j], send_sem=sh_s.at[j], recv_sem=sh_r.at[j],
            device_id=(after, x, z), device_id_type=MESH)

    def wait_shift():
        for j in range(nx):
            shift_copy(j).wait_recv()

    copies["x"].wait()
    copies["gain"].wait()
    first_normed = normalize(x_ref[...].astype(F32))
    for p in range(2):
        for j in range(nx):
            copies["win", p, j].wait()
    hyena_rows = layer(0, first_normed)
    for j in range(nx):
        cols = slice(j * cw, (j + 1) * cw)
        out = x_ref[:, cols].astype(F32) + (acc[:, cols] + dot(hyena_rows, exit_rows(1, j)))
        hsend[j] = out.astype(BF16)
        shift_copy(j).start()
    wait_sent(0)
    wait_shift()
    handed = jnp.concatenate([hrecv[j] for j in range(nx)], axis=1)
    head = lax.broadcast(sec, (LANES, d)) == 0
    second_in = jnp.where(head, emb[...].astype(F32), handed.astype(F32))
    emb[...] = second_in.astype(BF16)
    hyena_rows = layer(1, normalize(second_in))

    def z_copy(half, zz, to):
        return pltpu.make_async_remote_copy(
            src_ref=rsend.at[half, zz], dst_ref=rrecv.at[half, z if to else zz], send_sem=z_s.at[half, zz],
            recv_sem=z_r.at[half, z if to else zz], device_id=(sec, x, zz), device_id_type=MESH)

    def send_partials(half):
        rsend[half] = part[half].astype(BF16).reshape(nz, 16, d)

        def one(i, carry):
            z_copy(half, lax.rem(z + far(i), nz), True).start()
            return carry

        lax.fori_loop(0, nz - 1, one, 0)
        grad_ref[16 * half:16 * half + 16] = part[half, pl.ds(pl.multiple_of(z * 16, 16), 16), :]

    def add_partials(half):
        def one(i, carry):
            zz = lax.rem(z + i, nz)
            z_copy(half, zz, False).wait_recv()
            grad_ref[16 * half:16 * half + 16] = grad_ref[16 * half:16 * half + 16] + rrecv[half, zz].astype(F32)
            return carry

        lax.fori_loop(1, nz, one, 0)

    wait_y(1, 0)
    grad_of(1, 0)
    send_partials(0)
    for j in range(nx):
        cols = slice(j * cw, (j + 1) * cw)
        out = emb[:, cols].astype(F32) + (acc[:, cols] + dot(hyena_rows, exit_rows(1, j)))
        passed_ref[:, cols] = out.astype(BF16)
    wait_y(1, 1)
    grad_of(1, 1)
    send_partials(1)

    wait_sent(1)
    for j in range(nx):
        shift_copy(j).wait_send()
    for step in range(2):
        for w in range(2):
            seed_copy(step, w).wait_send()
            forward_copy(step, w).wait_send()
        for half in range(2):
            for o in range(1, nx):
                y_copy(step, half, lax.rem(x + o, nx), True).wait_send()
    add_partials(0)
    add_partials(1)

    def z_drain(i, carry):
        for half in range(2):
            z_copy(half, lax.rem(z + i, nz), True).wait_send()
        return carry

    lax.fori_loop(1, nz, z_drain, 0)


def local(shape, resident, ids, sizes, amino, poly, gain, win, kernels, skips, wout, seeds):
    ns, nx, nz = shape
    seq = nx * nz
    d = CH * seq
    cw = CH * nz
    hw = cw // 2
    fk, fi, tw, g = dft_tables(seq)
    vmem = pl.BlockSpec(memory_space=pltpu.VMEM)
    hbm = pl.BlockSpec(memory_space=pl.ANY)
    dma = pltpu.SemaphoreType.DMA
    operands = (resident[0], ids.reshape(1, LANES), sizes, amino, poly, gain, win[0], kernels[0], skips[0], wout[0],
                seeds[0], fk, fi, tw, g)

    def like(i, space=pltpu.VMEM):
        return space(operands[i].shape, operands[i].dtype)

    passed, grad = pl.pallas_call(
        lambda *refs: body(ns, nx, nz, *refs),
        out_shape=(jax.ShapeDtypeStruct((LANES, d), BF16), jax.ShapeDtypeStruct((CH, d), F32)),
        in_specs=[hbm] * len(operands),
        out_specs=(vmem, vmem),
        scratch_shapes=[
            like(0), like(1), like(2, pltpu.SMEM), like(3), like(4), like(5), like(8, pltpu.SMEM),
            like(11), like(12), like(13), like(14),
            pltpu.VMEM((3, nx, d, cw), BF16),
            pltpu.VMEM((nx, d, cw), BF16),
            pltpu.VMEM((2, CH, LANES * seq), F32),
            pltpu.VMEM((2, 4, 8 * seq, 2 * LANES), F32),
            pltpu.VMEM((2, nx, LANES, d), BF16),
            pltpu.VMEM((2, seq, 2, 16, LANES), BF16),
            pltpu.VMEM((2, seq, 2, 16, LANES), BF16),
            pltpu.VMEM((2, seq, 16, LANES), BF16),
            pltpu.VMEM((2, seq, 16, LANES), BF16),
            pltpu.VMEM((2, d // 2, LANES), BF16),
            pltpu.VMEM((2, 2, nx, hw, LANES), BF16),
            pltpu.VMEM((2, 2, nx, hw, LANES), BF16),
            pltpu.VMEM((nx, LANES, cw), BF16),
            pltpu.VMEM((nx, LANES, cw), BF16),
            pltpu.VMEM((LANES, d), BF16),
            pltpu.VMEM((LANES, d), F32),
            pltpu.VMEM((LANES, d), F32),
            pltpu.VMEM((2, hw, d), F32),
            pltpu.VMEM((2, nz, 16, d), BF16),
            pltpu.VMEM((2, nz, 16, d), BF16),
            dma((4 * nx + 14,)),
            dma((2, 2)),
            dma((2, 2)),
            dma((2, 2)),
            dma((2, 2)),
            dma((nx,)),
            dma((nx,)),
            dma((2, 2, nx)),
            dma((2, 2, nx)),
            dma((2, 2)),
            dma((2, 2)),
            dma((2, 2)),
            dma((2, 2)),
            dma((2, nz)),
            dma((2, nz)),
        ],
        compiler_params=pltpu.CompilerParams(
            collective_id=0, has_side_effects=True, vmem_limit_bytes=60 * 1024 * 1024),
    )(*operands)
    return passed[None], grad[None]


SEQ = ("seq_0", "seq_1")


def build(mesh, ns, nx, nz):
    torus = Mesh(mesh.devices.reshape(ns, nx, nz), ("section", "seq_0", "seq_1"))
    placed = (
        P("section", SEQ, None),
        P(SEQ),
        P(),
        P(),
        P(),
        P("section", None),
        P("section", None, None),
        P("section", None, SEQ, None),
        P("section", None, SEQ),
        P("section", None, None),
        P("section", None, SEQ, None),
    )
    return jax.shard_map(
        lambda *args: local((ns, nx, nz), *args),
        mesh=torus,
        in_specs=placed,
        out_specs=(P("section", SEQ, None), P("section", SEQ, None)),
        check_vma=False,
    )


def solution(mesh):
    return build(mesh, mesh.shape["section"], 4, 8)
```

time: 92.5 us -> 77.1 us (0.83)
  Pallas kernels: 88.4 us -> 72.9 us
    pallas_call x1, Pallas kernels: 88.4 us -> 72.9 us  [local(): pl.pallas_call(lambda *refs: body(ns, nx, nz, *refs), out_shape=(jax.Shap...]
where the time goes in v2:
time: 77.1 us; the launch traced here: 76.8 us
  Pallas kernels  72.9 us (95%)
  local copies, waits for them, and re-layouts  3.24 us (4%)
    pallas_call x1, Pallas kernels, local(): pl.pallas_call(lambda *refs: body(ns, nx, nz, *refs), out_shape=(jax.Shap...  72.9 us
    unnamed x2, local copies, waits for them, and re-layouts  3.24 us

profile of v2, /device:TPU:8, one launch (start us, length us, event | category | flops | bytes accessed | tf_op | source)
XLA Modules:
  0.0 76.8 jit_solution(17182894500379593329)
XLA Ops:
  0.6 72.9 %shard_map.158 = (bf16[128,1024]{1,0:T(8,128)(2,1)}, f32[32,1024]{1,0:T(8,128)}) custom-call(bf16[128,1024]{1,0:T(8,128)(2,1)} %bitcast.13, s32[1,128]{1,0:T(1,128)} %bitcast.17, s32[8]{0:T(128)} %refs_2_.1, bf16[32,1024]{1,0:T(8,128)(2,1)} %refs_3_.1, bf16[8,1024]{1,0:T(8,128)(2,1)} %refs_4_.1, f32[1,1024]{1,0:T(1,128)} %refs_5_.1, ...), custom_call_target="tpu_custom_call" | custom-call | tf_op jit(solution)/shard_map/pallas_call | solution.py:444
  73.6 1.7 %copy.19 = bf16[1,128,1024]{2,1,0:T(8,128)(2,1)} copy(bf16[1,128,1024]{2,1,0:T(8,128)(2,1)} %bitcast.14) | data formatting | bytes 524288
  75.3 1.6 %copy.20 = f32[1,32,1024]{2,1,0:T(8,128)} copy(f32[1,32,1024]{2,1,0:T(8,128)} %bitcast.15) | data formatting | bytes 262144

commit v3 on v2

--- a/solution.py
+++ b/solution.py
@@ -48,9 +48,9 @@
          seeds_hbm, fk_hbm, fi_hbm, tw_hbm, g_hbm,
          passed_ref, grad_ref,
          x_ref, ids_ref, sizes_ref, amino_ref, poly_ref, gain_ref, skip_ref, fk_ref, fi_ref, tw_ref, g_ref,
-         win, wout, h, spec, sall, vg_send, vg_recv, m_send, m_recv, g2t, hyt, yall, hsend, hrecv,
+         win, wout, h, spec, sall, vg_send, vg_recv, m_send, m_recv, m1_send, m1_recv, g2t, g2x, hyt, yall, hsend, hrecv,
          emb, tab, acc, part, rsend, rrecv,
-         lsem, vg_s, vg_r, m_s, m_r, sh_s, sh_r, y_s, y_r, s_s, s_r, f_s, f_r, z_s, z_r):
+         lsem, vg_s, vg_r, m_s, m_r, m1_s, m1_r, m2_s, m2_r, g2_s, g2_r, sh_s, sh_r, y_s, y_r, s_s, s_r, f_s, f_r, z_s, z_r):
     seq = nx * nz
     d = CH * seq
     cw = CH * nz
@@ -124,26 +124,82 @@
             dst[me] = src[me]
 
     def wait_all(ref, sem):
-        block = ref.at[pl.ds(0, seq - 1)]
+        block = ref.at[pl.ds(0, ref.shape[0] - 1)]
         pltpu.make_async_copy(block, block, sem).wait()
 
     def send_vg(k, half, o):
         send_column(o, vg_send.at[half], vg_recv.at[half], vg_s.at[k, half], vg_r.at[k, half])
 
     def send_mixed(k, half):
+        if k == 0:
+            for o in orders:
+                send_column(o, m_send.at[half], m_recv.at[half], m_s.at[half], m_r.at[half])
+        else:
+            send_along_z(half)
+
+    def send_along_z(half):
+        def one(i, carry):
+            zz = lax.rem(z + far(i), nz)
+            pltpu.make_async_remote_copy(
+                src_ref=m1_send.at[half, zz], dst_ref=m1_recv.at[half, z], send_sem=m1_s.at[half],
+                recv_sem=m1_r.at[half], device_id=(sec, x, zz), device_id_type=MESH).start()
+            return carry
+
+        lax.fori_loop(0, nz - 1, one, 0)
+        m1_recv[half, z] = m1_send[half, z]
+
+    def wait_along_z(half):
+        wait_all(m1_recv.at[half], m1_r.at[half])
+
+    def on_copy(half, xx, to):
+        return pltpu.make_async_remote_copy(
+            src_ref=m1_recv.at[half, :, xx], dst_ref=m_recv.at[half, pl.ds((x if to else xx) * nz, nz)],
+            send_sem=m2_s.at[half, xx], recv_sem=m2_r.at[half, x if to else xx],
+            device_id=(sec, xx, z), device_id_type=MESH)
+
+    def send_on(half):
         for o in orders:
-            send_column(o, m_send.at[half], m_recv.at[half], m_s.at[k, half], m_r.at[k, half])
+            if o:
+                on_copy(half, lax.rem(x + o, nx), True).start()
+        m_recv[half, pl.ds(x * nz, nz)] = m1_recv[half, :, x]
+
+    def gate_copy(xx, to):
+        return pltpu.make_async_remote_copy(
+            src_ref=g2t.at[xx], dst_ref=g2x.at[x if to else xx], send_sem=g2_s.at[xx],
+            recv_sem=g2_r.at[x if to else xx], device_id=(sec, xx, z), device_id_type=MESH)
+
+    def send_gates():
+        for o in orders:
+            if o:
+                gate_copy(lax.rem(x + o, nx), True).start()
+        g2x[x] = g2t[x]
+
+    def wait_gates():
+        for o in range(1, nx):
+            gate_copy(lax.rem(x + o, nx), False).wait_recv()
+
+    def hyena_along_x(half):
+        for j in range(nx):
+            y = m1_recv[half, :, j].reshape(hw, LANES).astype(F32) * g2x[j, half].astype(F32)
+            yall[1, half, j] = y.astype(BF16)
 
     def wait_vg(k, half):
         wait_all(vg_recv.at[half], vg_r.at[k, half])
 
     def wait_mixed(k, half):
-        wait_all(m_recv.at[half], m_r.at[k, half])
+        if k == 0:
+            wait_all(m_recv.at[half], m_r.at[half])
+        else:
+            for o in range(1, nx):
+                on_copy(half, lax.rem(x + o, nx), False).wait_recv()
 
     def wait_sent(k):
         for half in range(2):
             wait_all(vg_send.at[half], vg_s.at[k, half])
-            wait_all(m_send.at[half], m_s.at[k, half])
+            if k == 0:
+                wait_all(m_send.at[half], m_s.at[half])
+            else:
+                wait_all(m1_send.at[half], m1_s.at[half])
 
     def along_x(ref, send_sem, recv_sem, direction):
         return pltpu.make_async_remote_copy(
@@ -199,14 +255,19 @@
         gains = jnp.concatenate([skip_tile(f, 2 * pair), skip_tile(f, 2 * pair + 1)], axis=1)
         return y + (xin.reshape(seq, 8, 2 * LANES) * gains[None]).reshape(rows, 2 * LANES)
 
-    def convolve(pair):
+    def convolve(k, pair):
         v = rows_of(pair, 0)
         y = with_skip(long_filter(v.astype(BF16), 0, pair), 0, pair, v)
         gated = rows_of(pair, 1) * y
         y = with_skip(long_filter(gated.astype(BF16), 1, pair), 1, pair, gated)
         y = y.reshape(seq, 8, 2 * LANES)
         out = jnp.concatenate([y[:, :, :LANES], y[:, :, LANES:]], axis=1)
-        m_send[pair] = out.astype(BF16)
+        out = out.astype(BF16)
+        if k == 0:
+            m_send[pair] = out
+        else:
+            for j in range(nx):
+                m1_send[pair, :, j] = out[j * nz:(j + 1) * nz]
 
     def filter_spectra(f, pair):
         scale = 1.0 / (LANES * seq)
@@ -245,26 +306,27 @@
     def project_gate(j, normed):
         chunk = dot(normed, win[2, j]).T.astype(BF16).reshape(per, 2, 16, LANES)
         for half in range(2):
-            g2t[half, pl.ds(j * hw, hw)] = chunk[:, half].reshape(hw, LANES)
-
-    def y_copy(step, half, xx, to):
+            g2t[j, half] = chunk[:, half].reshape(hw, LANES)
+
+    def y_copy(half, xx, to):
         return pltpu.make_async_remote_copy(
-            src_ref=hyt.at[step, half, xx], dst_ref=yall.at[step, half, x if to else xx],
-            send_sem=y_s.at[step, half, xx], recv_sem=y_r.at[step, half, x if to else xx],
+            src_ref=hyt.at[half, xx], dst_ref=yall.at[0, half, x if to else xx],
+            send_sem=y_s.at[half, xx], recv_sem=y_r.at[half, x if to else xx],
             device_id=(sec, xx, z), device_id_type=MESH)
 
     def make_hyena(k, half):
-        hyena = m_recv[half].reshape(d // 2, LANES).astype(F32) * g2t[half].astype(F32)
-        hyt[k, half] = hyena.astype(BF16).reshape(nx, hw, LANES)
-        for o in orders:
-            if o:
-                y_copy(k, half, lax.rem(x + o, nx), True).start()
-        yall[k, half, x] = hyt[k, half, x]
+        hyena = m_recv[half].reshape(d // 2, LANES).astype(F32) * g2t[:, half].reshape(d // 2, LANES).astype(F32)
+        if k == 0:
+            hyt[half] = hyena.astype(BF16).reshape(nx, hw, LANES)
+            for o in orders:
+                if o:
+                    y_copy(half, lax.rem(x + o, nx), True).start()
+            yall[0, half, x] = hyt[half, x]
         return hyena.T.astype(BF16)
 
-    def wait_y(step, half):
+    def wait_y(half):
         for o in range(1, nx):
-            y_copy(step, half, lax.rem(x + o, nx), False).wait_recv()
+            y_copy(half, lax.rem(x + o, nx), False).wait_recv()
 
     def grad_of(step, half):
         y = jnp.concatenate([yall[step, half, j] for j in range(nx)], axis=1)
@@ -289,6 +351,40 @@
     def normalize(values):
         return (values * lax.rsqrt(jnp.mean(values * values, axis=1, keepdims=True) + EPS) * gain_ref[...]).astype(BF16)
 
+    def z_copy(half, zz, to):
+        return pltpu.make_async_remote_copy(
+            src_ref=rsend.at[half, zz], dst_ref=rrecv.at[half, z if to else zz], send_sem=z_s.at[half, zz],
+            recv_sem=z_r.at[half, z if to else zz], device_id=(sec, x, zz), device_id_type=MESH)
+
+    def send_partials(half):
+        rsend[half] = part[half].astype(BF16).reshape(nz, 16, d)
+
+        def one(i, carry):
+            z_copy(half, lax.rem(z + far(i), nz), True).start()
+            return carry
+
+        lax.fori_loop(0, nz - 1, one, 0)
+        grad_ref[16 * half:16 * half + 16] = part[half, pl.ds(pl.multiple_of(z * 16, 16), 16), :]
+
+    def add_partials(half):
+        def one(i, carry):
+            zz = lax.rem(z + i, nz)
+            z_copy(half, zz, False).wait_recv()
+            grad_ref[16 * half:16 * half + 16] = grad_ref[16 * half:16 * half + 16] + rrecv[half, zz].astype(F32)
+            return carry
+
+        lax.fori_loop(1, nz, one, 0)
+
+    def send_seeds(step):
+        copies["seed", step].wait()
+        seed_copy(step, 0).start()
+        seed_copy(step, 1).start()
+
+    def forward_seeds(step):
+        for w in range(2):
+            seed_arrival(step, w).wait_recv()
+            forward_copy(step, w).start()
+
     def layer(k, normed):
         for o in orders:
             xx = lax.rem(x + o, nx)
@@ -299,16 +395,15 @@
             send_vg(k, 0, o)
         for o in orders:
             send_vg(k, 1, o)
-        if k == 1:
-            for step in range(2):
-                for w in range(2):
-                    seed_arrival(step, w).wait_recv()
-                    forward_copy(step, w).start()
-        else:
+        if k == 0:
+            send_seeds(0)
             for j in range(nx):
                 copies["win", 2, j].wait()
         for j in range(nx):
             project_gate(j, normed)
+        if k == 1:
+            send_gates()
+            forward_seeds(1)
         if k == 0:
             for name in ("h", "fk", "tw", "g", "fi", "skip", "ids", "sizes", "amino", "poly"):
                 copies[name].wait()
@@ -318,13 +413,10 @@
             embed()
         for half in range(2):
             wait_vg(k, half)
-            convolve(half)
+            convolve(k, half)
             send_mixed(k, half)
         if k == 0:
-            for step in range(2):
-                copies["seed", step].wait()
-                seed_copy(step, 0).start()
-                seed_copy(step, 1).start()
+            send_seeds(1)
             for j in range(nx):
                 copies["wout", j].wait()
         else:
@@ -332,13 +424,23 @@
                 for w in range(2):
                     forward_arrival(step, w).wait_recv()
             for half in range(2):
-                wait_y(0, half)
+                wait_y(half)
                 grad_of(0, half)
+            wait_gates()
+            for half in range(2):
+                wait_along_z(half)
+                send_on(half)
+                hyena_along_x(half)
+                grad_of(1, half)
+                send_partials(half)
         wait_mixed(k, 0)
         first_rows = make_hyena(k, 0)
         half_exit(first_rows)
         wait_mixed(k, 1)
-        return make_hyena(k, 1)
+        second_rows = make_hyena(k, 1)
+        if k == 0:
+            forward_seeds(0)
+        return second_rows
 
     def shift_copy(j):
         return pltpu.make_async_remote_copy(
@@ -369,41 +471,10 @@
     emb[...] = second_in.astype(BF16)
     hyena_rows = layer(1, normalize(second_in))
 
-    def z_copy(half, zz, to):
-        return pltpu.make_async_remote_copy(
-            src_ref=rsend.at[half, zz], dst_ref=rrecv.at[half, z if to else zz], send_sem=z_s.at[half, zz],
-            recv_sem=z_r.at[half, z if to else zz], device_id=(sec, x, zz), device_id_type=MESH)
-
-    def send_partials(half):
-        rsend[half] = part[half].astype(BF16).reshape(nz, 16, d)
-
-        def one(i, carry):
-            z_copy(half, lax.rem(z + far(i), nz), True).start()
-            return carry
-
-        lax.fori_loop(0, nz - 1, one, 0)
-        grad_ref[16 * half:16 * half + 16] = part[half, pl.ds(pl.multiple_of(z * 16, 16), 16), :]
-
-    def add_partials(half):
-        def one(i, carry):
-            zz = lax.rem(z + i, nz)
-            z_copy(half, zz, False).wait_recv()
-            grad_ref[16 * half:16 * half + 16] = grad_ref[16 * half:16 * half + 16] + rrecv[half, zz].astype(F32)
-            return carry
-
-        lax.fori_loop(1, nz, one, 0)
-
-    wait_y(1, 0)
-    grad_of(1, 0)
-    send_partials(0)
     for j in range(nx):
         cols = slice(j * cw, (j + 1) * cw)
         out = emb[:, cols].astype(F32) + (acc[:, cols] + dot(hyena_rows, exit_rows(1, j)))
         passed_ref[:, cols] = out.astype(BF16)
-    wait_y(1, 1)
-    grad_of(1, 1)
-    send_partials(1)
-
     wait_sent(1)
     for j in range(nx):
         shift_copy(j).wait_send()
@@ -411,9 +482,12 @@
         for w in range(2):
             seed_copy(step, w).wait_send()
             forward_copy(step, w).wait_send()
+    for o in range(1, nx):
+        xx = lax.rem(x + o, nx)
+        gate_copy(xx, True).wait_send()
         for half in range(2):
-            for o in range(1, nx):
-                y_copy(step, half, lax.rem(x + o, nx), True).wait_send()
+            y_copy(half, xx, True).wait_send()
+            on_copy(half, xx, True).wait_send()
     add_partials(0)
     add_partials(1)
 
@@ -443,7 +517,7 @@
 
     passed, grad = pl.pallas_call(
         lambda *refs: body(ns, nx, nz, *refs),
-        out_shape=(jax.ShapeDtypeStruct((LANES, d), BF16), jax.ShapeDtypeStruct((CH, d), F32)),
+        out_shape=(pltpu.VMEM((LANES, d), BF16), pltpu.VMEM((CH, d), F32)),
         in_specs=[hbm] * len(operands),
         out_specs=(vmem, vmem),
         scratch_shapes=[
@@ -458,8 +532,11 @@
             pltpu.VMEM((2, seq, 2, 16, LANES), BF16),
             pltpu.VMEM((2, seq, 16, LANES), BF16),
             pltpu.VMEM((2, seq, 16, LANES), BF16),
-            pltpu.VMEM((2, d // 2, LANES), BF16),
-            pltpu.VMEM((2, 2, nx, hw, LANES), BF16),
+            pltpu.VMEM((2, nz, nx, 16, LANES), BF16),
+            pltpu.VMEM((2, nz, nx, 16, LANES), BF16),
+            pltpu.VMEM((nx, 2, hw, LANES), BF16),
+            pltpu.VMEM((nx, 2, hw, LANES), BF16),
+            pltpu.VMEM((2, nx, hw, LANES), BF16),
             pltpu.VMEM((2, 2, nx, hw, LANES), BF16),
             pltpu.VMEM((nx, LANES, cw), BF16),
             pltpu.VMEM((nx, LANES, cw), BF16),
@@ -472,12 +549,18 @@
             dma((4 * nx + 14,)),
             dma((2, 2)),
             dma((2, 2)),
-            dma((2, 2)),
-            dma((2, 2)),
+            dma((2,)),
+            dma((2,)),
+            dma((2,)),
+            dma((2,)),
+            dma((2, nx)),
+            dma((2, nx)),
             dma((nx,)),
             dma((nx,)),
-            dma((2, 2, nx)),
-            dma((2, 2, nx)),
+            dma((nx,)),
+            dma((nx,)),
+            dma((2, nx)),
+            dma((2, nx)),
             dma((2, 2)),
             dma((2, 2)),
             dma((2, 2)),
@@ -486,7 +569,7 @@
             dma((2, nz)),
         ],
         compiler_params=pltpu.CompilerParams(
-            collective_id=0, has_side_effects=True, vmem_limit_bytes=60 * 1024 * 1024),
+            collective_id=0, has_side_effects=True, vmem_limit_bytes=66600000),
     )(*operands)
     return passed[None], grad[None]
 

time: 77.1 us -> 70.9 us (0.920)
  Pallas kernels: 72.9 us -> 68.3 us
  local copies, waits for them, and re-layouts: 3.24 us -> 1.36 us
    pallas_call x1, Pallas kernels: 72.9 us -> 68.3 us  [local(): pl.pallas_call(lambda *refs: body(ns, nx, nz, *refs), out_shape=(pltpu.VM...]
    unnamed x2, local copies, waits for them, and re-layouts: 3.24 us -> 1.36 us
where the time goes in v3:
time: 70.9 us; the launch traced here: 70.3 us
  Pallas kernels  68.3 us (96%)
  local copies, waits for them, and re-layouts  1.36 us (2%)
    pallas_call x1, Pallas kernels, local(): pl.pallas_call(lambda *refs: body(ns, nx, nz, *refs), out_shape=(pltpu.VM...  68.3 us

profile of v3, /device:TPU:8, one launch (start us, length us, event | category | flops | bytes accessed | tf_op | source)
XLA Modules:
  0.0 70.3 jit_solution(73271790764186306)
XLA Ops:
  0.6 68.3 %shard_map.158 = (bf16[128,1024]{1,0:T(8,128)(2,1)S(1)}, f32[32,1024]{1,0:T(8,128)S(1)}) custom-call(bf16[128,1024]{1,0:T(8,128)(2,1)} %bitcast.15, s32[1,128]{1,0:T(1,128)} %bitcast.17, s32[8]{0:T(128)} %refs_2_.1, bf16[32,1024]{1,0:T(8,128)(2,1)} %refs_3_.1, bf16[8,1024]{1,0:T(8,128)(2,1)} %refs_4_.1, f32[1,1024]{1,0:T(1,128)} %refs_5_.1, ...), custom_call_target="tpu_custom_call" | custom-call | tf_op jit(solution)/shard_map/pallas_call | solution.py:518
  68.9 0.7 %copy.19 = bf16[1,128,1024]{2,1,0:T(8,128)(2,1)} copy(bf16[1,128,1024]{2,1,0:T(8,128)(2,1)S(1)} %bitcast.9) | data formatting | bytes 524288
  69.6 0.7 copy.20

commit v4 on v3

--- a/solution.py
+++ b/solution.py
@@ -48,9 +48,9 @@
          seeds_hbm, fk_hbm, fi_hbm, tw_hbm, g_hbm,
          passed_ref, grad_ref,
          x_ref, ids_ref, sizes_ref, amino_ref, poly_ref, gain_ref, skip_ref, fk_ref, fi_ref, tw_ref, g_ref,
-         win, wout, h, spec, sall, vg_send, vg_recv, m_send, m_recv, m1_send, m1_recv, g2t, g2x, hyt, yall, hsend, hrecv,
+         win, wout, h, spec, sall, vg_send, vg_recv, w_send, w_recv, m_send, m_recv, m1_send, m1_recv, g2t, g2x, hyt, yall, hsend, hrecv,
          emb, tab, acc, part, rsend, rrecv,
-         lsem, vg_s, vg_r, m_s, m_r, m1_s, m1_r, m2_s, m2_r, g2_s, g2_r, sh_s, sh_r, y_s, y_r, s_s, s_r, f_s, f_r, z_s, z_r):
+         lsem, vg_s, vg_r, w_s, w_r, m_s, m_r, m1_s, m1_r, m2_s, m2_r, g2_s, g2_r, sh_s, sh_r, y_s, y_r, s_s, s_r, f_s, f_r, z_s, z_r):
     seq = nx * nz
     d = CH * seq
     cw = CH * nz
@@ -67,23 +67,36 @@
         copies[name] = pltpu.make_async_copy(src, dst, lsem.at[len(copies)])
         copies[name].start()
 
+    def far(i):
+        half = (i + 1) // 2
+        return nz // 2 + half * (1 - 2 * lax.rem(i, 2))
+
+    orders = [o % nx for o in (2, 1, 3, 0)]
+    columns = [lax.rem(x + o, nx) for o in orders]
+
+    barrier = pltpu.get_barrier_semaphore()
+
+    def greet(dev):
+        pl.semaphore_signal(barrier, inc=1, device_id=dev, device_id_type=MESH)
+
     fetch("x", x_hbm, x_ref)
+    for xx, o in zip(columns, orders):
+        def one(i, carry, xx=xx):
+            greet((sec, xx, lax.rem(z + far(i), nz)))
+            return carry
+
+        lax.fori_loop(0, nz - 1, one, 0)
+        if o:
+            greet((sec, xx, z))
+    greet((after, x, z))
+    greet((before, x, z))
+
     fetch("gain", gain_hbm, gain_ref)
-    for p in range(3):
-        for j in range(nx):
-            fetch(("win", p, j), win_hbm.at[:, pl.ds((p * nx + j) * cw, cw)], win.at[p, j])
-
-    barrier = pltpu.get_barrier_semaphore()
-
-    def greet(i, carry):
-        peer = lax.rem(me + i, seq)
-        pl.semaphore_signal(barrier, inc=1, device_id=(sec, peer // nz, lax.rem(peer, nz)), device_id_type=MESH)
-        return carry
-
-    pl.semaphore_signal(barrier, inc=1, device_id=(after, x, z), device_id_type=MESH)
-    pl.semaphore_signal(barrier, inc=1, device_id=(before, x, z), device_id_type=MESH)
-    lax.fori_loop(1, seq, greet, 0)
-
+    for xx, o in zip(columns, orders):
+        for p in range(2):
+            fetch(("win", p, o), win_hbm.at[:, pl.ds(pl.multiple_of((p * nx + xx) * cw, cw), cw)], win.at[p, xx])
+    for j in range(nx):
+        fetch(("win", 2, j), win_hbm.at[:, pl.ds((2 * nx + j) * cw, cw)], win.at[2, j])
     fetch("fk", fk_hbm, fk_ref)
     fetch("tw", tw_hbm, tw_ref)
     fetch("g", g_hbm, g_ref)
@@ -99,12 +112,6 @@
     for j in range(nx):
         fetch(("wout", j), wout_hbm.at[:, pl.ds(j * cw, cw)], wout.at[j])
 
-    def far(i):
-        half = (i + 1) // 2
-        return nz // 2 + half * (1 - 2 * lax.rem(i, 2))
-
-    orders = [o % nx for o in (2, 1, 3, 0)]
-
     def block_to(peer, src, dst, send_sem, recv_sem):
         pltpu.make_async_remote_copy(
             src_ref=src.at[peer], dst_ref=dst.at[me], send_sem=send_sem, recv_sem=recv_sem,
@@ -127,8 +134,12 @@
         block = ref.at[pl.ds(0, ref.shape[0] - 1)]
         pltpu.make_async_copy(block, block, sem).wait()
 
-    def send_vg(k, half, o):
-        send_column(o, vg_send.at[half], vg_recv.at[half], vg_s.at[k, half], vg_r.at[k, half])
+    def send_vg(k, o):
+        send_column(o, vg_send, vg_recv, vg_s.at[k], vg_r.at[k])
+
+    def send_w(k, p):
+        for o in orders:
+            send_column(o, w_send.at[p], w_recv.at[p], w_s.at[k, p], w_r.at[k, p])
 
     def send_mixed(k, half):
         if k == 0:
@@ -183,8 +194,11 @@
             y = m1_recv[half, :, j].reshape(hw, LANES).astype(F32) * g2x[j, half].astype(F32)
             yall[1, half, j] = y.astype(BF16)
 
-    def wait_vg(k, half):
-        wait_all(vg_recv.at[half], vg_r.at[k, half])
+    def wait_vg(k):
+        wait_all(vg_recv, vg_r.at[k])
+
+    def wait_w(k, p):
+        wait_all(w_recv.at[p], w_r.at[k, p])
 
     def wait_mixed(k, half):
         if k == 0:
@@ -194,8 +208,9 @@
                 on_copy(half, lax.rem(x + o, nx), False).wait_recv()
 
     def wait_sent(k):
+        wait_all(vg_send, vg_s.at[k])
         for half in range(2):
-            wait_all(vg_send.at[half], vg_s.at[k, half])
+            wait_all(w_send.at[half], w_s.at[k, half])
             if k == 0:
                 wait_all(m_send.at[half], m_s.at[half])
             else:
@@ -241,7 +256,7 @@
         return dot(fi_ref[...], jnp.concatenate(cols, axis=1))
 
     def rows_of(half, which):
-        v = vg_recv[half, :, which].astype(F32)
+        v = (w_recv[which] if half else vg_recv[:, which]).astype(F32)
         return jnp.concatenate([v[:, :8, :].reshape(rows, LANES), v[:, 8:, :].reshape(rows, LANES)], axis=1)
 
     def skip_tile(f, group):
@@ -256,8 +271,14 @@
         return y + (xin.reshape(seq, 8, 2 * LANES) * gains[None]).reshape(rows, 2 * LANES)
 
     def convolve(k, pair):
+        if pair:
+            wait_w(k, 0)
+        else:
+            wait_vg(k)
         v = rows_of(pair, 0)
         y = with_skip(long_filter(v.astype(BF16), 0, pair), 0, pair, v)
+        if pair:
+            wait_w(k, 1)
         gated = rows_of(pair, 1) * y
         y = with_skip(long_filter(gated.astype(BF16), 1, pair), 1, pair, gated)
         y = y.reshape(seq, 8, 2 * LANES)
@@ -300,8 +321,8 @@
 
     def project(p, xx, normed):
         chunk = dot(normed, win[p, xx]).T.astype(BF16).reshape(per, 2, 16, LANES)
-        for half in range(2):
-            vg_send[half, pl.ds(xx * per, per), p] = chunk[:, half]
+        vg_send[pl.ds(xx * per, per), p] = chunk[:, 0]
+        w_send[p, pl.ds(xx * per, per)] = chunk[:, 1]
 
     def project_gate(j, normed):
         chunk = dot(normed, win[2, j]).T.astype(BF16).reshape(per, 2, 16, LANES)
@@ -380,21 +401,26 @@
         seed_copy(step, 0).start()
         seed_copy(step, 1).start()
 
+    def wait_seeds(step):
+        for w in range(2):
+            forward_arrival(step, w).wait_recv()
+
     def forward_seeds(step):
         for w in range(2):
             seed_arrival(step, w).wait_recv()
             forward_copy(step, w).start()
 
     def layer(k, normed):
-        for o in orders:
-            xx = lax.rem(x + o, nx)
-            project(0, xx, normed)
-            project(1, xx, normed)
+        for xx, o in zip(columns, orders):
+            for p in range(2):
+                if k == 0:
+                    copies["win", p, o].wait()
+                project(p, xx, normed)
             if k == 0 and o == orders[0]:
                 pl.semaphore_wait(barrier, seq + 1)
-            send_vg(k, 0, o)
-        for o in orders:
-            send_vg(k, 1, o)
+            send_vg(k, o)
+        for p in range(2):
+            send_w(k, p)
         if k == 0:
             send_seeds(0)
             for j in range(nx):
@@ -403,7 +429,7 @@
             project_gate(j, normed)
         if k == 1:
             send_gates()
-            forward_seeds(1)
+            forward_seeds(0)
         if k == 0:
             for name in ("h", "fk", "tw", "g", "fi", "skip", "ids", "sizes", "amino", "poly"):
                 copies[name].wait()
@@ -412,34 +438,35 @@
                     filter_spectra(f, pair)
             embed()
         for half in range(2):
-            wait_vg(k, half)
             convolve(k, half)
             send_mixed(k, half)
+            if k == 1 and half == 0:
+                forward_seeds(1)
         if k == 0:
             send_seeds(1)
             for j in range(nx):
                 copies["wout", j].wait()
         else:
-            for step in range(2):
-                for w in range(2):
-                    forward_arrival(step, w).wait_recv()
-            for half in range(2):
-                wait_y(half)
-                grad_of(0, half)
+            wait_seeds(0)
+            wait_y(0)
+            grad_of(0, 0)
             wait_gates()
             for half in range(2):
                 wait_along_z(half)
                 send_on(half)
                 hyena_along_x(half)
+                if half == 0:
+                    wait_seeds(1)
                 grad_of(1, half)
                 send_partials(half)
+                if half == 0:
+                    wait_y(1)
+                    grad_of(0, 1)
         wait_mixed(k, 0)
         first_rows = make_hyena(k, 0)
         half_exit(first_rows)
         wait_mixed(k, 1)
         second_rows = make_hyena(k, 1)
-        if k == 0:
-            forward_seeds(0)
         return second_rows
 
     def shift_copy(j):
@@ -447,37 +474,43 @@
             src_ref=hsend.at[j], dst_ref=hrecv.at[j], send_sem=sh_s.at[j], recv_sem=sh_r.at[j],
             device_id=(after, x, z), device_id_type=MESH)
 
+    def start_shift(j):
+        @pl.when(sec < ns - 1)
+        def _():
+            shift_copy(j).start()
+
     def wait_shift():
-        for j in range(nx):
-            shift_copy(j).wait_recv()
+        @pl.when(sec > 0)
+        def _():
+            for j in range(nx):
+                shift_copy(j).wait_recv()
+            emb[...] = jnp.concatenate([hrecv[j] for j in range(nx)], axis=1)
 
     copies["x"].wait()
     copies["gain"].wait()
     first_normed = normalize(x_ref[...].astype(F32))
-    for p in range(2):
-        for j in range(nx):
-            copies["win", p, j].wait()
     hyena_rows = layer(0, first_normed)
-    for j in range(nx):
-        cols = slice(j * cw, (j + 1) * cw)
-        out = x_ref[:, cols].astype(F32) + (acc[:, cols] + dot(hyena_rows, exit_rows(1, j)))
-        hsend[j] = out.astype(BF16)
-        shift_copy(j).start()
+    for j in range(0, nx, 2):
+        cols = slice(j * cw, (j + 2) * cw)
+        w = jnp.concatenate([exit_rows(1, j), exit_rows(1, j + 1)], axis=1)
+        out = (x_ref[:, cols].astype(F32) + (acc[:, cols] + dot(hyena_rows, w))).astype(BF16)
+        for i in range(2):
+            hsend[j + i] = out[:, i * cw:(i + 1) * cw]
+            start_shift(j + i)
     wait_sent(0)
     wait_shift()
-    handed = jnp.concatenate([hrecv[j] for j in range(nx)], axis=1)
-    head = lax.broadcast(sec, (LANES, d)) == 0
-    second_in = jnp.where(head, emb[...].astype(F32), handed.astype(F32))
-    emb[...] = second_in.astype(BF16)
-    hyena_rows = layer(1, normalize(second_in))
+    hyena_rows = layer(1, normalize(emb[...].astype(F32)))
 
     for j in range(nx):
         cols = slice(j * cw, (j + 1) * cw)
         out = emb[:, cols].astype(F32) + (acc[:, cols] + dot(hyena_rows, exit_rows(1, j)))
         passed_ref[:, cols] = out.astype(BF16)
     wait_sent(1)
-    for j in range(nx):
-        shift_copy(j).wait_send()
+    @pl.when(sec < ns - 1)
+    def _():
+        for j in range(nx):
+            shift_copy(j).wait_send()
+
     for step in range(2):
         for w in range(2):
             seed_copy(step, w).wait_send()
@@ -528,8 +561,10 @@
             pltpu.VMEM((2, CH, LANES * seq), F32),
             pltpu.VMEM((2, 4, 8 * seq, 2 * LANES), F32),
             pltpu.VMEM((2, nx, LANES, d), BF16),
-            pltpu.VMEM((2, seq, 2, 16, LANES), BF16),
-            pltpu.VMEM((2, seq, 2, 16, LANES), BF16),
+            pltpu.VMEM((seq, 2, 16, LANES), BF16),
+            pltpu.VMEM((seq, 2, 16, LANES), BF16),
+            pltpu.VMEM((2, seq, 16, LANES), BF16),
+            pltpu.VMEM((2, seq, 16, LANES), BF16),
             pltpu.VMEM((2, seq, 16, LANES), BF16),
             pltpu.VMEM((2, seq, 16, LANES), BF16),
             pltpu.VMEM((2, nz, nx, 16, LANES), BF16),
@@ -547,6 +582,8 @@
             pltpu.VMEM((2, nz, 16, d), BF16),
             pltpu.VMEM((2, nz, 16, d), BF16),
             dma((4 * nx + 14,)),
+            dma((2,)),
+            dma((2,)),
             dma((2, 2)),
             dma((2, 2)),
             dma((2,)),
@@ -571,7 +608,22 @@
         compiler_params=pltpu.CompilerParams(
             collective_id=0, has_side_effects=True, vmem_limit_bytes=66600000),
     )(*operands)
-    return passed[None], grad[None]
+
+    def write(passed_ref, grad_ref, passed_out, grad_out, sems):
+        copies = [pltpu.make_async_copy(passed_ref, passed_out.at[0], sems.at[0]),
+                  pltpu.make_async_copy(grad_ref, grad_out.at[0], sems.at[1])]
+        for c in copies:
+            c.start()
+        for c in copies:
+            c.wait()
+
+    return pl.pallas_call(
+        write,
+        out_shape=(jax.ShapeDtypeStruct((1, LANES, d), BF16), jax.ShapeDtypeStruct((1, CH, d), F32)),
+        in_specs=[vmem, vmem],
+        out_specs=(hbm, hbm),
+        scratch_shapes=[dma((2,))],
+    )(*(pltpu.with_memory_space_constraint(t, pltpu.VMEM) for t in (passed, grad)))
 
 
 SEQ = ("seq_0", "seq_1")

time: 70.9 us -> 69.5 us (0.980)
  local copies, waits for them, and re-layouts: 1.36 us -> 0 us
    unnamed x2 -> x0, local copies, waits for them, and re-layouts: 1.36 us -> none
    pallas_call x0 -> x1, Pallas kernels: none -> 0.76 us  [local(): pl.pallas_call(write, out_shape=(jax.ShapeDtypeStruct((1, LANES, d), BF16...]
where the time goes in v4:
time: 69.5 us; the launch traced here: 69.3 us
  Pallas kernels  68.7 us (99%)
    pallas_call x1, Pallas kernels, local(): pl.pallas_call(lambda *refs: body(ns, nx, nz, *refs), out_shape=(pltpu.VM...  67.9 us

profile of v4, /device:TPU:8, one launch (start us, length us, event | category | flops | bytes accessed | tf_op | source)
XLA Modules:
  0.0 69.3 jit_solution(7108273698101287188)
XLA Ops:
  0.6 67.9 %shard_map.158 = (bf16[128,1024]{1,0:T(8,128)(2,1)S(1)}, f32[32,1024]{1,0:T(8,128)S(1)}) custom-call(bf16[128,1024]{1,0:T(8,128)(2,1)} %bitcast.11, s32[1,128]{1,0:T(1,128)} %bitcast.13, s32[8]{0:T(128)} %refs_2_.1, bf16[32,1024]{1,0:T(8,128)(2,1)} %refs_3_.1, bf16[8,1024]{1,0:T(8,128)(2,1)} %refs_4_.1, f32[1,1024]{1,0:T(1,128)} %refs_5_.1, ...), custom_call_target="tpu_custom_call" | custom-call | tf_op jit(solution)/shard_map/pallas_call | solution.py:551
  68.6 0.8 %shard_map.159 = (bf16[1,128,1024]{2,1,0:T(8,128)(2,1)}, f32[1,32,1024]{2,1,0:T(8,128)}) custom-call(bf16[128,1024]{1,0:T(8,128)(2,1)S(1)} %get-tuple-element.4.passed_ref, f32[32,1024]{1,0:T(8,128)S(1)} %get-tuple-element.5.grad_ref), custom_call_target="tpu_custom_call" | custom-call | tf_op jit(solution)/shard_map/pallas_call | solution.py:620

commit v5 on v4

--- a/solution.py
+++ b/solution.py
@@ -417,7 +417,10 @@
                     copies["win", p, o].wait()
                 project(p, xx, normed)
             if k == 0 and o == orders[0]:
+                continue
+            if k == 0 and o == orders[1]:
                 pl.semaphore_wait(barrier, seq + 1)
+                send_vg(k, orders[0])
             send_vg(k, o)
         for p in range(2):
             send_w(k, p)

time: 69.5 us -> 69.8 us (level)
  no operation moved by 1% of the time
where the time goes in v5:
time: 69.8 us; the launch traced here: 69.7 us
  Pallas kernels  69 us (99%)
    pallas_call x1, Pallas kernels, local(): pl.pallas_call(lambda *refs: body(ns, nx, nz, *refs), out_shape=(pltpu.VM...  68.3 us

profile of v5, /device:TPU:8, one launch (start us, length us, event | category | flops | bytes accessed | tf_op | source)
XLA Modules:
  0.0 69.7 jit_solution(7250559351963201863)
XLA Ops:
  0.6 68.3 %shard_map.158 = (bf16[128,1024]{1,0:T(8,128)(2,1)S(1)}, f32[32,1024]{1,0:T(8,128)S(1)}) custom-call(bf16[128,1024]{1,0:T(8,128)(2,1)} %bitcast.11, s32[1,128]{1,0:T(1,128)} %bitcast.13, s32[8]{0:T(128)} %refs_2_.1, bf16[32,1024]{1,0:T(8,128)(2,1)} %refs_3_.1, bf16[8,1024]{1,0:T(8,128)(2,1)} %refs_4_.1, f32[1,1024]{1,0:T(1,128)} %refs_5_.1, ...), custom_call_target="tpu_custom_call" | custom-call | tf_op jit(solution)/shard_map/pallas_call | solution.py:554
  68.9 0.8 %shard_map.159 = (bf16[1,128,1024]{2,1,0:T(8,128)(2,1)}, f32[1,32,1024]{2,1,0:T(8,128)}) custom-call(bf16[128,1024]{1,0:T(8,128)(2,1)S(1)} %get-tuple-element.4.passed_ref, f32[32,1024]{1,0:T(8,128)S(1)} %get-tuple-element.5.grad_ref), custom_call_target="tpu_custom_call" | custom-call | tf_op jit(solution)/shard_map/pallas_call | solution.py:623
